TPU v7x, 32 devices: a whole 2x2x4 slice. The times are simulated.
32 devices in a mesh: face: 4 (over x, core), sub: 8 (over z, y).
Axes of the slice: x: 2, y: 2, z: 4, core: 2. Of those that a mesh axis runs over, the one named last changes fastest.
Arguments:
- grid_inputs: bfloat16 [131072, 474], P(('face', 'sub')), may hold values from -6 to 6
- mesh_nodes: bfloat16 [10240, 512], P(('face', 'sub')), may hold values from -6 to 6
- encoder_edges: bfloat16 [4, 256, 512], P(None, ('face', 'sub')), may hold values from -6 to 6
- mesh_edges: bfloat16 [4, 81920], P(None, ('face', 'sub')), may hold values from -6 to 6
- grid_send: int32 [256, 512], P(('face', 'sub')), may hold values from -1 to 4095, as said below
- node_receive: int32 [256, 512], P(('face', 'sub')), may hold values from -1 to 319, as said below
- halo_send: int32 [1024, 16], P(('face', 'sub')), may hold values from -1 to 319, as said below
- edge_source: int32 [81920], P(('face', 'sub')), may hold values from 0 to 831, as said below
- edge_target: int32 [81920], P(('face', 'sub')), may hold values from 0 to 319
- embed_first: bfloat16 [474, 512], replicated, may hold values from -0.09186304 to 0.09186304
- embed_second: bfloat16 [512, 512], replicated, may hold values from -0.088388348 to 0.088388348
- encoder_feature: bfloat16 [4, 512], replicated, may hold values from -1.75 to 1.75
- encoder_sender: bfloat16 [512, 512], replicated, may hold values from -0.05103104 to 0.05103104
- encoder_receiver: bfloat16 [512, 512], replicated, may hold values from -0.15625 to 0.15625
- encoder_output: bfloat16 [512, 512], replicated, may hold values from -0.25 to 0.25
- updater_self: bfloat16 [512, 512], replicated, may hold values from -0.1875 to 0.1875
- updater_message: bfloat16 [512, 512], replicated, may hold values from -0.1875 to 0.1875
- updater_output: bfloat16 [512, 512], replicated, may hold values from -0.25 to 0.25
- processor_feature: bfloat16 [4, 512], replicated, may hold values from -1.75 to 1.75
- processor_sender: bfloat16 [512, 512], replicated, may hold values from -0.05103104 to 0.05103104
- processor_receiver: bfloat16 [512, 512], replicated, may hold values from -0.15625 to 0.15625
- processor_output: bfloat16 [512, 512], replicated, may hold values from -0.25 to 0.25
- refiner_self: bfloat16 [512, 512], replicated, may hold values from -0.1875 to 0.1875
- refiner_message: bfloat16 [512, 512], replicated, may hold values from -0.1875 to 0.1875
- refiner_output: bfloat16 [512, 512], replicated, may hold values from -0.25 to 0.25
Outputs:
- mesh_state: bfloat16 [10240, 512], P(('face', 'sub'))
Inputs may be any that keep to these rules, and one draw needn't show every extreme that they name: `grid_send`: on tile (f, s), row r lists up to 512 slots of grid-to-mesh edges toward tile (f, r); the used slots of a row come first, -1 marks an empty slot. In every face group one tile receives full rows from all 8 sources. `node_receive`: on tile (f, r), entry [s, k] is the receiving local mesh node of the edge in slot k of row r of grid_send on tile (f, s); -1 exactly where that slot is empty. `halo_send`: on tile p, row q lists up to 16 local mesh nodes that tile q reads; used slots come first, -1 marks an empty slot, row p is empty. One tile receives full rows from every other tile. `edge_source`: index into the receiving tile's table of its 320 nodes followed by the 32 x 16 slots sent to it, source-major (slot k from tile p at 320 + p * 16 + k). Every used slot sent to a tile is read by exactly one of its edges; no empty slot is read.
All inputs are finite; a program needn't handle non-finite values.
Results may differ from a plain program's by a relative error of at most 0.0095.
Values may be sent and summed in bfloat16 or wider, within the bound.
A program may use at most 128 MiB of HBM per device.

v0:
```python
import functools

import jax
import jax.numpy as jnp
from jax import lax
from jax.experimental import pallas as pl
from jax.experimental.pallas import tpu as pltpu
from jax.sharding import PartitionSpec as P

EPSILON = 1e-05
LANES = 128
MESH_ID = pl.DeviceIdType.MESH


def silu(values):
    half = values * 0.5
    return (half + half * jnp.tanh(half)).astype(jnp.bfloat16)


def norm(values):
    width = values.shape[-1]
    centered = values - jnp.sum(values, axis=-1, keepdims=True) * (1.0 / width)
    spread = jnp.sum(centered * centered, axis=-1, keepdims=True) * (1.0 / width)
    return centered * lax.rsqrt(spread + EPSILON)


def dot(a, b):
    return jnp.dot(a, b, preferred_element_type=jnp.float32)


def dot_t(a, b):
    return lax.dot_general(a, b, (((0,), (0,)), ((), ())), preferred_element_type=jnp.float32)


def pick(count, index):
    rows = lax.broadcasted_iota(jnp.int32, (count, index.shape[1]), 0)
    return jnp.where(rows == index, 1.0, 0.0).astype(jnp.bfloat16)


def sub_at(position, subs):
    position = lax.rem(position + subs, subs)
    return jnp.where(position < subs // 2, 2 * position, 2 * (subs - 1 - position) + 1)


def ring_position(subs):
    sub = lax.axis_index("sub")
    return jnp.where(lax.rem(sub, 2) == 0, sub // 2, subs - 1 - sub // 2)


def ring_order(subs):
    order = []
    for distance in range(1, subs // 2):
        order += [subs - distance, distance]
    return order + [subs // 2, 0]


def device_at(position, subs):
    return (lax.axis_index("face"), sub_at(position, subs))


def embed_kernel(
    chunk,
    subs,
    index_ref,
    x_ref,
    first_ref,
    second_ref,
    sender_ref,
    nodes_ref,
    aux_ref,
    out_ref,
    nodes_out,
    aux_out,
    table,
    slots,
    slot_sem,
    own_sem,
    ring_send,
    ring_recv,
    aux_send,
    aux_recv,
):
    step = pl.program_id(0)
    steps = pl.num_programs(0)
    rows, width = x_ref.shape[1], second_ref.shape[1]
    nodes, half = nodes_ref.shape[0], nodes_ref.shape[0] // 2
    parts = width // LANES
    capacity = index_ref.shape[1]
    order = ring_order(subs)
    place_of = {distance: place for place, distance in enumerate(order)}
    here = ring_position(subs)

    def ring(flow, hop):
        sign = 1 - 2 * flow
        span = pl.ds(flow * half, half)
        old = place_of[(-sign * hop) % subs]
        new = place_of[(-sign * (hop + 1)) % subs]
        return pltpu.make_async_remote_copy(
            src_ref=nodes_ref.at[span, :] if hop == 0 else nodes_out.at[old, span, :],
            dst_ref=nodes_out.at[new, span, :],
            send_sem=ring_send.at[flow, hop],
            recv_sem=ring_recv.at[flow, hop],
            device_id=device_at(here + sign, subs),
            device_id_type=MESH_ID,
        )

    def side(distance):
        return pltpu.make_async_remote_copy(
            src_ref=aux_ref.at[sub_at(here + distance, subs)],
            dst_ref=aux_out.at[place_of[subs - distance]],
            send_sem=aux_send.at[distance],
            recv_sem=aux_recv.at[distance],
            device_id=device_at(here + distance, subs),
            device_id_type=MESH_ID,
        )

    def own():
        place = place_of[0]
        return (
            pltpu.make_async_copy(nodes_ref, nodes_out.at[place], own_sem.at[0]),
            pltpu.make_async_copy(aux_ref.at[sub_at(here, subs)], aux_out.at[place], own_sem.at[1]),
        )

    def forward(hop):
        for flow in range(2):
            ring(flow, hop - 1).wait_recv()
            ring(flow, hop).start()

    @pl.when(step == 0)
    def _():
        barrier = pltpu.get_barrier_semaphore()
        for distance in range(1, subs):
            pl.semaphore_signal(
                barrier, inc=1, device_id=device_at(here + distance, subs), device_id_type=MESH_ID
            )
        pl.semaphore_wait(barrier, subs - 1)
        for flow in range(2):
            ring(flow, 0).start()
        for distance in range(1, subs):
            side(distance).start()
        for copy in own():
            copy.start()

    hidden = silu(dot_t(x_ref[...], first_ref[...]))
    latent = norm(dot(hidden, second_ref[...])).astype(jnp.bfloat16)
    sent = dot(latent, sender_ref[...])
    base = pl.multiple_of(step * rows, rows)
    for part in range(parts):
        table[pl.ds(base, rows), part, :] = sent[:, part * LANES : (part + 1) * LANES]

    @pl.when(step == steps // 2 - 1)
    def _():
        forward(1)

    @pl.when(step == steps - 1)
    def _():
        forward(2)
        done = 2

        def move(place):
            return pltpu.make_async_copy(slots.at[place], out_ref.at[place], slot_sem.at[place])

        for place, distance in enumerate(order):
            target = sub_at(here + distance, subs)

            @pl.loop(0, capacity // chunk)
            def _(block):
                for slot in range(chunk):
                    spot = block * chunk + slot
                    slots[place, spot] = table[index_ref[target, spot]]

            move(place).start()
            while done < 2 + ((place + 1) * (subs - 4)) // subs:
                done += 1
                forward(done)
        for flow in range(2):
            ring(flow, subs - 2).wait_recv()
            for hop in range(subs - 1):
                ring(flow, hop).wait_send()
        for distance in range(1, subs):
            side(distance).wait()
        for copy in own():
            copy.wait()
        for place in range(subs):
            move(place).wait()


def edge_kernel(
    block,
    subs,
    sent_ref,
    nodes_ref,
    aux_ref,
    receiver_ref,
    feature_ref,
    output_ref,
    out_ref,
    acc,
    table,
    kept,
    outbox,
    inbox,
    ring_send,
    ring_recv,
):
    step = pl.program_id(0)
    nodes, width = nodes_ref.shape[1], nodes_ref.shape[2]
    half = nodes // 2
    capacity = aux_ref.shape[2]
    parts = width // LANES
    order = ring_order(subs)
    here = ring_position(subs)

    @pl.when(step == 0)
    def _():
        barrier = pltpu.get_barrier_semaphore()
        for distance in (1, subs - 1):
            pl.semaphore_signal(
                barrier, inc=1, device_id=device_at(here + distance, subs), device_id_type=MESH_ID
            )

    table[:nodes, :] = dot(nodes_ref[0], receiver_ref[...]).astype(jnp.bfloat16)
    table[nodes:, :] = feature_ref[...]
    aux = aux_ref[0]
    values = aux[:8, :].astype(jnp.float32)
    index = (values[4:5, :] * 16.0 + values[5:6, :]).astype(jnp.int32)
    for start in range(0, capacity, block):
        chosen = pick(nodes, index[:, start : start + block])
        wide = jnp.concatenate([chosen, aux[:, start : start + block]], axis=0)
        sent = jnp.concatenate(
            [
                sent_ref[0, start : start + block, part, :]
                for part in range(parts)
            ],
            axis=1,
        )
        summed = dot_t(wide, table[...]) + sent
        message = norm(dot(silu(summed), output_ref[...])).astype(jnp.bfloat16)
        if start == 0:
            acc[...] = dot(chosen, message)
        else:
            acc[...] += dot(chosen, message)
    kept[step] = acc[...].astype(jnp.bfloat16)

    def ring(flow, hop):
        sign = 1 - 2 * flow
        return pltpu.make_async_remote_copy(
            src_ref=outbox.at[flow, hop],
            dst_ref=inbox.at[flow, hop],
            send_sem=ring_send.at[flow, hop],
            recv_sem=ring_recv.at[flow, hop],
            device_id=device_at(here + sign, subs),
            device_id_type=MESH_ID,
        )

    def push(flow, hop):
        sign = 1 - 2 * flow
        place = order.index((-sign * (hop + 1)) % subs)
        own = kept[place, flow * half : (flow + 1) * half, :]
        if hop == 0:
            outbox[flow, hop] = own
        else:
            ring(flow, hop - 1).wait_recv()
            total = own.astype(jnp.float32) + inbox[flow, hop - 1].astype(jnp.float32)
            outbox[flow, hop] = total.astype(jnp.bfloat16)
        ring(flow, hop).start()

    for place in range(subs):
        distance = order[place]

        @pl.when(step == place)
        def _():
            if place == 0:
                pl.semaphore_wait(pltpu.get_barrier_semaphore(), 2)
            if distance == 0:
                for hop in range(subs // 2, subs - 1):
                    for flow in range(2):
                        push(flow, hop)
                for flow in range(2):
                    ring(flow, subs - 2).wait_recv()
                    span = slice(flow * half, (flow + 1) * half)
                    total = acc[span, :] + inbox[flow, subs - 2].astype(jnp.float32)
                    out_ref[span, :] = total.astype(jnp.bfloat16)
                for flow in range(2):
                    for hop in range(subs - 1):
                        ring(flow, hop).wait_send()
            elif distance == subs // 2:
                for flow in range(2):
                    push(flow, distance - 1)
            elif distance > subs // 2:
                push(0, subs - distance - 1)
            else:
                push(1, distance - 1)


def processor_kernel(
    block,
    faces,
    subs,
    nodes_ref,
    sum_ref,
    halo_ref,
    source_ref,
    target_ref,
    edges_ref,
    feature_ref,
    *rest,
):
    weights, rest = rest[:9], rest[9:]
    (
        out_ref,
        held,
        held_sem,
        outgoing,
        arrived,
        local_table,
        summed,
        acc,
        send_sem,
        recv_sem,
    ) = rest

    def fetch(place):
        return pltpu.make_async_copy(weights[place], held.at[place], held_sem.at[place])

    for place in range(len(weights)):
        fetch(place).start()

    def weight(place):
        fetch(place).wait()
        return held[place]

    devices = faces * subs
    me = lax.axis_index("face") * subs + lax.axis_index("sub")
    nodes, width = nodes_ref.shape
    slots = halo_ref.shape[1] // devices
    edges = source_ref.shape[1]
    barrier = pltpu.get_barrier_semaphore()

    @pl.loop(1, devices)
    def _(step):
        other = lax.rem(me + step, devices)
        pl.semaphore_signal(
            barrier, inc=1, device_id=(other // subs, lax.rem(other, subs)), device_id_type=MESH_ID
        )

    start = nodes_ref[...]
    before = dot(start, weight(0)) + dot(sum_ref[...], weight(1))
    refined = norm(dot(silu(before), weight(2)))
    state = (start.astype(jnp.float32) + refined).astype(jnp.bfloat16)
    outgoing[...] = dot_t(pick(nodes, halo_ref[...]), state).astype(jnp.bfloat16)
    arrived[pl.ds(pl.multiple_of(me * slots, slots), slots), :] = jnp.zeros(
        (slots, width), jnp.bfloat16
    )
    pl.semaphore_wait(barrier, devices - 1)

    def copy(step):
        other = lax.rem(me + step, devices)
        return pltpu.make_async_remote_copy(
            src_ref=outgoing.at[pl.ds(pl.multiple_of(other * slots, slots), slots), :],
            dst_ref=arrived.at[pl.ds(pl.multiple_of(me * slots, slots), slots), :],
            send_sem=send_sem.at[step],
            recv_sem=recv_sem.at[step],
            device_id=(other // subs, lax.rem(other, subs)),
            device_id_type=MESH_ID,
        )

    @pl.loop(1, devices)
    def _(step):
        copy(step).start()

    local_table[:nodes, :] = dot(state, weight(3)).astype(jnp.bfloat16)
    local_table[nodes : 2 * nodes, :] = dot(state, weight(4)).astype(jnp.bfloat16)
    local_table[2 * nodes :, :] = feature_ref[...]
    own_part = dot(state, weight(6))
    for first in range(0, edges, block):
        span = slice(first, first + block)
        wide = jnp.concatenate(
            [
                pick(nodes, source_ref[:, span]),
                pick(nodes, target_ref[:, span]),
                edges_ref[:, span],
            ],
            axis=0,
        )
        summed[span, :] = dot_t(wide, local_table[...])

    @pl.loop(1, devices)
    def _(step):
        copy(step).wait()

    remote_table = dot(arrived[...], held[3]).astype(jnp.bfloat16)
    acc[...] = jnp.zeros_like(acc)
    fetch(5).wait()
    for first in range(0, edges, block):
        span = slice(first, first + block)
        remote = pick(devices * slots, source_ref[:, span] - nodes)
        total = summed[span, :] + dot_t(remote, remote_table)
        message = norm(dot(silu(total), held[5])).astype(jnp.bfloat16)
        acc[...] += dot(pick(nodes, target_ref[:, span]), message)
    after = own_part + dot(acc[...].astype(jnp.bfloat16), weight(7))
    final = norm(dot(silu(after), weight(8)))
    out_ref[...] = (state.astype(jnp.float32) + final).astype(jnp.bfloat16)


def vmem():
    return pl.BlockSpec(memory_space=pltpu.VMEM)


def smem():
    return pl.BlockSpec(memory_space=pltpu.SMEM)


def shards(
    grid_inputs,
    mesh_nodes,
    encoder_edges,
    mesh_edges,
    grid_send,
    node_receive,
    halo_send,
    edge_source,
    edge_target,
    embed_first,
    embed_second,
    encoder_feature,
    encoder_sender,
    encoder_receiver,
    encoder_output,
    updater_self,
    updater_message,
    updater_output,
    processor_feature,
    processor_sender,
    processor_receiver,
    processor_output,
    refiner_self,
    refiner_message,
    refiner_output,
):
    subs = lax.axis_size("sub")
    faces = lax.axis_size("face")
    devices = subs * faces
    grid_rows, inputs = grid_inputs.shape
    nodes, width = mesh_nodes.shape
    capacity = grid_send.shape[1]
    parts = width // LANES
    feats = encoder_edges.shape[0]

    receive = jnp.stack([node_receive >> 4, node_receive & 15]).astype(jnp.bfloat16)
    aux = jnp.concatenate(
        [encoder_edges, receive, jnp.zeros((16 - feats - 2, subs, capacity), jnp.bfloat16)], axis=0
    ).transpose(1, 0, 2)
    rows = 512
    whole = lambda shape: pl.BlockSpec(shape, lambda i: (0,) * len(shape))
    anywhere = pl.BlockSpec(memory_space=pl.ANY)
    sent, face_nodes, face_aux = pl.pallas_call(
        functools.partial(embed_kernel, min(64, capacity), subs),
        grid=(grid_rows // rows,),
        out_shape=(
            jax.ShapeDtypeStruct((subs, capacity, parts, LANES), jnp.float32),
            jax.ShapeDtypeStruct((subs, nodes, width), jnp.bfloat16),
            jax.ShapeDtypeStruct((subs, 16, capacity), jnp.bfloat16),
        ),
        in_specs=[
            smem(),
            pl.BlockSpec((inputs, rows), lambda i: (0, i)),
            whole((inputs, width)),
            whole((width, width)),
            whole((width, width)),
            vmem(),
            vmem(),
        ],
        out_specs=(anywhere, anywhere, anywhere),
        scratch_shapes=[
            pltpu.VMEM((grid_rows, parts, LANES), jnp.float32),
            pltpu.VMEM((subs, capacity, parts, LANES), jnp.float32),
            pltpu.SemaphoreType.DMA((subs,)),
            pltpu.SemaphoreType.DMA((2,)),
            pltpu.SemaphoreType.DMA((2, subs - 1)),
            pltpu.SemaphoreType.DMA((2, subs - 1)),
            pltpu.SemaphoreType.DMA((subs,)),
            pltpu.SemaphoreType.DMA((subs,)),
        ],
        compiler_params=pltpu.CompilerParams(
            collective_id=1, has_side_effects=True, vmem_limit_bytes=56 * 2**20
        ),
        name="embed",
    )(
        jnp.maximum(grid_send, 0),
        grid_inputs.T,
        embed_first,
        embed_second,
        encoder_sender,
        mesh_nodes,
        aux,
    )

    pad_feature = lambda weight: jnp.pad(weight, ((0, 16 - feats), (0, 0)))
    mine = lambda shape: pl.BlockSpec((1,) + shape, lambda i: (i, 0, 0))
    half = nodes // 2
    summed = pl.pallas_call(
        functools.partial(edge_kernel, min(256, capacity), subs),
        grid=(subs,),
        in_specs=[
            pl.BlockSpec((1, capacity, parts, LANES), lambda i: (i, 0, 0, 0)),
            mine((nodes, width)),
            mine((16, capacity)),
            whole((width, width)),
            whole((16, width)),
            whole((width, width)),
        ],
        out_specs=whole((nodes, width)),
        scratch_shapes=[
            pltpu.VMEM((nodes, width), jnp.float32),
            pltpu.VMEM((nodes + 16, width), jnp.bfloat16),
            pltpu.VMEM((subs, nodes, width), jnp.bfloat16),
            pltpu.VMEM((2, subs - 1, half, width), jnp.bfloat16),
            pltpu.VMEM((2, subs - 1, half, width), jnp.bfloat16),
            pltpu.SemaphoreType.DMA((2, subs - 1)),
            pltpu.SemaphoreType.DMA((2, subs - 1)),
        ],
        out_shape=jax.ShapeDtypeStruct((nodes, width), jnp.bfloat16),
        compiler_params=pltpu.CompilerParams(
            collective_id=2, has_side_effects=True, vmem_limit_bytes=60 * 2**20
        ),
        name="edges",
    )(sent, face_nodes, face_aux, encoder_receiver, pad_feature(encoder_feature), encoder_output)

    edge_count = edge_source.shape[0]
    halo = halo_send.reshape(1, -1)
    step = min(512, edge_count)
    operands = (
        mesh_nodes,
        summed,
        halo,
        edge_source.reshape(1, -1),
        edge_target.reshape(1, -1),
        jnp.pad(mesh_edges, ((0, 16 - feats), (0, 0))),
        pad_feature(processor_feature),
        updater_self,
        updater_message,
        updater_output,
        processor_sender,
        processor_receiver,
        processor_output,
        refiner_self,
        refiner_message,
        refiner_output,
    )
    return pl.pallas_call(
        functools.partial(processor_kernel, step, faces, subs),
        out_shape=jax.ShapeDtypeStruct((nodes, width), jnp.bfloat16),
        in_specs=[vmem()] * (len(operands) - 9) + [anywhere] * 9,
        out_specs=vmem(),
        scratch_shapes=[
            pltpu.VMEM((9, width, width), jnp.bfloat16),
            pltpu.SemaphoreType.DMA((9,)),
            pltpu.VMEM((halo.shape[1], width), jnp.bfloat16),
            pltpu.VMEM((halo.shape[1], width), jnp.bfloat16),
            pltpu.VMEM((2 * nodes + 16, width), jnp.bfloat16),
            pltpu.VMEM((edge_count, width), jnp.float32),
            pltpu.VMEM((nodes, width), jnp.float32),
            pltpu.SemaphoreType.DMA((devices,)),
            pltpu.SemaphoreType.DMA((devices,)),
        ],
        compiler_params=pltpu.CompilerParams(
            collective_id=0, has_side_effects=True, vmem_limit_bytes=60 * 2**20
        ),
        name="processor",
    )(*operands)


def solution(mesh):
    rows = P(("face", "sub"), None)
    placed = (
        rows,
        rows,
        P(None, ("face", "sub"), None),
        P(None, ("face", "sub")),
        rows,
        rows,
        rows,
        P(("face", "sub")),
        P(("face", "sub")),
    ) + (P(),) * 16
    return jax.shard_map(
        shards, mesh=mesh, in_specs=placed, out_specs=P(("face", "sub"), None), check_vma=False
    )
```

profile of v0, /device:TPU:0, one launch (start us, length us, event | category | flops | bytes accessed | tf_op | source)
XLA Modules:
  0.0 129.5 jit_solution(5272161111297544177)
XLA Ops:
  0.0 0.0 copy-start.4
  0.0 0.7 fusion
  0.8 0.8 copy.28
  1.6 0.1 pad.17.clone
  1.6 0.7 maximum_bitcast_fusion.aux_ref
  2.4 1.3 %broadcast_maximum_fusion.index_ref = s32[8,512]{1,0:T(8,128)} fusion(s32[8,512]{1,0:T(8,128)} %param.29), kind=kLoop, calls=%fused_computation.5 | loop fusion | flops 4096 | bytes 32768 | tf_op jit(solution)/shard_map/max | solution.py:490
  3.7 48.5 %embed.1 = (f32[8,512,4,128]{3,2,1,0:T(4,128)}, bf16[8,320,512]{2,1,0:T(8,128)(2,1)}, bf16[8,16,512]{2,1,0:T(8,128)(2,1)}) custom-call(s32[8,512]{1,0:T(8,128)} %broadcast_maximum_fusion.index_ref, bf16[474,4096]{1,0:T(8,128)(2,1)} %bitcast.7, bf16[474,512]{1,0:T(8,128)(2,1)} %first_ref.1, bf16[512,512]{1,0:T(8,128)(2,1)} %second_ref.1, ...), custom_call_target="tpu_custom_call" | custom-call | tf_op jit(solution)/shard_map/embed/pallas_call | solution.py:457
  52.3 0.0 copy-done.4
  52.3 0.6 pad.11.feature_ref
  52.9 0.0 copy-start
  52.9 0.0 copy-start.3
  52.9 0.0 copy-start.5
  52.9 0.0 copy-start.1
  52.9 0.0 copy-start.2
  52.9 43.2 %edges.1.sum_ref = bf16[320,512]{1,0:T(8,128)(2,1)} custom-call(f32[8,512,4,128]{3,2,1,0:T(4,128)} %get-tuple-element.8.sent_ref, bf16[8,320,512]{2,1,0:T(8,128)(2,1)} %get-tuple-element.9.nodes_ref, bf16[8,16,512]{2,1,0:T(8,128)(2,1)} %get-tuple-element.10.aux_ref, bf16[512,512]{1,0:T(8,128)(2,1)} %receiver_ref.1, bf16[16,512]{1,0:T(8,128)(2,1)} %pad.11.feature_ref, ...), custom_call_target="tpu_custom_call" | custom-call | tf_op jit(solution)/shard_map/edges/pallas_call | solution.py:502
  96.1 0.0 copy-done
  96.1 0.6 pad.12.edges_ref
  96.7 0.0 copy-done.3
  96.7 0.1 copy.31
  96.8 0.7 reshape.9.halo_ref
  97.5 0.0 copy-done.5
  97.5 0.6 pad.13.feature_ref
  98.1 0.0 copy-done.1
  98.1 0.6 reshape.10.source_ref
  98.7 0.0 copy-done.2
  98.7 0.6 reshape.11.target_ref
  99.3 28.5 %processor.1 = bf16[320,512]{1,0:T(8,128)(2,1)} custom-call(bf16[320,512]{1,0:T(8,128)(2,1)} %nodes_ref.3, bf16[320,512]{1,0:T(8,128)(2,1)} %edges.1.sum_ref, s32[1,512]{1,0:T(1,128)} %reshape.9.halo_ref, s32[1,2560]{1,0:T(1,128)} %reshape.10.source_ref, s32[1,2560]{1,0:T(1,128)} %reshape.11.target_ref, bf16[16,2560]{1,0:T(8,128)(2,1)} %pad.12.edges_ref, ...), custom_call_target="tpu_custom_call" | custom-call | tf_op jit(solution)/shard_map/processor/pallas_call | solution.py:551
  127.8 1.7 %copy.33 = bf16[320,512]{1,0:T(8,128)(2,1)} copy(bf16[320,512]{1,0:T(8,128)(2,1)} %processor.1) | data formatting | bytes 655360
  (3 shorter events, 0.0 us)
Async XLA Ops:
  0.0 52.3 %copy-start.4 = (bf16[4,512]{1,0:T(4,128)(2,1)S(1)}, bf16[4,512]{1,0:T(4,128)(2,1)}, u32[]{:S(2)}) copy-start(bf16[4,512]{1,0:T(4,128)(2,1)} %param.36) | copy-start | bytes 12292
  52.9 43.2 %copy-start = (bf16[4,2560]{1,0:T(4,128)(2,1)S(1)}, bf16[4,2560]{1,0:T(4,128)(2,1)}, u32[]{:S(2)}) copy-start(bf16[4,2560]{1,0:T(4,128)(2,1)} %param.28) | copy-start | bytes 61444
  52.9 43.8 %copy-start.3 = (s32[32,16]{0,1:T(8,128)S(1)}, s32[32,16]{0,1:T(8,128)}, u32[]{:S(2)}) copy-start(s32[32,16]{0,1:T(8,128)} %param.31) | copy-start | bytes 6148
  52.9 44.6 %copy-start.5 = (bf16[4,512]{1,0:T(4,128)(2,1)S(1)}, bf16[4,512]{1,0:T(4,128)(2,1)}, u32[]{:S(2)}) copy-start(bf16[4,512]{1,0:T(4,128)(2,1)} %param.43) | copy-start | bytes 12292
  52.9 45.2 %copy-start.1 = (s32[2560]{0:T(1024)S(1)}, s32[2560]{0:T(1024)}, u32[]{:S(2)}) copy-start(s32[2560]{0:T(1024)} %param.32) | copy-start | bytes 30724
  52.9 45.8 %copy-start.2 = (s32[2560]{0:T(1024)S(1)}, s32[2560]{0:T(1024)}, u32[]{:S(2)}) copy-start(s32[2560]{0:T(1024)} %param.33) | copy-start | bytes 30724
where the time goes:
time: 130 us
  Pallas kernels  120 us (92%)
  local copies, waits for them, and re-layouts  6.43 us (5%)
  other arithmetic  2.8 us (2%)
    pallas_call x1, Pallas kernels, shards(): pl.pallas_call(functools.partial(embed_kernel, min(64, capacity), subs),...  48.5 us
    pallas_call x1, Pallas kernels, shards(): pl.pallas_call(functools.partial(edge_kernel, min(256, capacity), subs),...  43.2 us
    pallas_call x1, Pallas kernels, shards(): pl.pallas_call(functools.partial(processor_kernel, step, faces, subs), ou...  28.5 us

commit v1 on v0

--- a/solution.py
+++ b/solution.py
@@ -293,6 +293,19 @@
                 push(1, distance - 1)
 
 
+def partner(step, faces, subs):
+    face, sub = lax.axis_index("face"), lax.axis_index("sub")
+    return flip(face, lax.rem(step, faces), faces), flip(sub, step // faces, subs)
+
+
+def flip(index, mask, count):
+    total, bit = 0, 1
+    while bit < count:
+        total = total + lax.rem(lax.rem(index // bit, 2) + lax.rem(mask // bit, 2), 2) * bit
+        bit *= 2
+    return total
+
+
 def processor_kernel(
     block,
     faces,
@@ -314,7 +327,7 @@
         outgoing,
         arrived,
         local_table,
-        summed,
+        base,
         acc,
         send_sem,
         recv_sem,
@@ -334,15 +347,14 @@
     me = lax.axis_index("face") * subs + lax.axis_index("sub")
     nodes, width = nodes_ref.shape
     slots = halo_ref.shape[1] // devices
+    table_slots = devices * slots
     edges = source_ref.shape[1]
     barrier = pltpu.get_barrier_semaphore()
 
     @pl.loop(1, devices)
     def _(step):
-        other = lax.rem(me + step, devices)
-        pl.semaphore_signal(
-            barrier, inc=1, device_id=(other // subs, lax.rem(other, subs)), device_id_type=MESH_ID
-        )
+        face, sub = partner(step, faces, subs)
+        pl.semaphore_signal(barrier, inc=1, device_id=(face, sub), device_id_type=MESH_ID)
 
     start = nodes_ref[...]
     before = dot(start, weight(0)) + dot(sum_ref[...], weight(1))
@@ -355,24 +367,53 @@
     pl.semaphore_wait(barrier, devices - 1)
 
     def copy(step):
-        other = lax.rem(me + step, devices)
+        face, sub = partner(step, faces, subs)
+        other = face * subs + sub
         return pltpu.make_async_remote_copy(
             src_ref=outgoing.at[pl.ds(pl.multiple_of(other * slots, slots), slots), :],
             dst_ref=arrived.at[pl.ds(pl.multiple_of(me * slots, slots), slots), :],
             send_sem=send_sem.at[step],
             recv_sem=recv_sem.at[step],
-            device_id=(other // subs, lax.rem(other, subs)),
+            device_id=(face, sub),
             device_id_type=MESH_ID,
         )
 
     @pl.loop(1, devices)
     def _(step):
-        copy(step).start()
+        copy(devices - step).start()
 
     local_table[:nodes, :] = dot(state, weight(3)).astype(jnp.bfloat16)
     local_table[nodes : 2 * nodes, :] = dot(state, weight(4)).astype(jnp.bfloat16)
     local_table[2 * nodes :, :] = feature_ref[...]
     own_part = dot(state, weight(6))
+
+    group = min(512, table_slots)
+    source = source_ref[...]
+    target = target_ref[...]
+    tags = edges_ref[...]
+    high = (target // 16).astype(jnp.float32)
+    low = (target - (target // 16) * 16).astype(jnp.float32)
+    digits = jnp.concatenate(
+        [high, low, jnp.ones_like(high), jnp.zeros((13, edges), jnp.float32)], axis=0
+    ).astype(jnp.bfloat16)
+    info = jnp.concatenate([tags, digits], axis=0)
+    spots = []
+    for first in range(0, table_slots, group):
+        rows = lax.broadcasted_iota(jnp.int32, (group, edges), 0) + (nodes + first)
+        reads = jnp.where(rows == source, 1.0, 0.0).astype(jnp.bfloat16)
+        found = lax.dot_general(
+            reads, info, (((1,), (1,)), ((), ())), preferred_element_type=jnp.float32
+        )
+        spot = found[:, 16:17] * 16.0 + found[:, 17:18] + found[:, 18:19] - 1.0
+        spot = spot.astype(jnp.int32)
+        lanes = lax.broadcasted_iota(jnp.int32, (group, nodes), 1)
+        chosen = jnp.where(lanes == spot, 1.0, 0.0).astype(jnp.bfloat16)
+        base[first : first + group, :] = dot(chosen, local_table[nodes : 2 * nodes, :]) + dot(
+            found[:, :16].astype(jnp.bfloat16), local_table[2 * nodes :, :]
+        )
+        spots.append(chosen)
+
+    fetch(5).wait()
     for first in range(0, edges, block):
         span = slice(first, first + block)
         wide = jnp.concatenate(
@@ -383,21 +424,23 @@
             ],
             axis=0,
         )
-        summed[span, :] = dot_t(wide, local_table[...])
+        total = dot_t(wide, local_table[...])
+        message = norm(dot(silu(total), held[5])).astype(jnp.bfloat16)
+        kept = jnp.where(source_ref[:, span] < nodes, target_ref[:, span], -1)
+        if first == 0:
+            acc[...] = dot(pick(nodes, kept), message)
+        else:
+            acc[...] += dot(pick(nodes, kept), message)
 
     @pl.loop(1, devices)
     def _(step):
-        copy(step).wait()
-
-    remote_table = dot(arrived[...], held[3]).astype(jnp.bfloat16)
-    acc[...] = jnp.zeros_like(acc)
-    fetch(5).wait()
-    for first in range(0, edges, block):
-        span = slice(first, first + block)
-        remote = pick(devices * slots, source_ref[:, span] - nodes)
-        total = summed[span, :] + dot_t(remote, remote_table)
+        copy(devices - step).wait()
+
+    for place, first in enumerate(range(0, table_slots, group)):
+        span = slice(first, first + group)
+        total = base[span, :] + dot(arrived[span, :], held[3])
         message = norm(dot(silu(total), held[5])).astype(jnp.bfloat16)
-        acc[...] += dot(pick(nodes, target_ref[:, span]), message)
+        acc[...] += dot_t(spots[place], message)
     after = own_part + dot(acc[...].astype(jnp.bfloat16), weight(7))
     final = norm(dot(silu(after), weight(8)))
     out_ref[...] = (state.astype(jnp.float32) + final).astype(jnp.bfloat16)
@@ -559,7 +602,7 @@
             pltpu.VMEM((halo.shape[1], width), jnp.bfloat16),
             pltpu.VMEM((halo.shape[1], width), jnp.bfloat16),
             pltpu.VMEM((2 * nodes + 16, width), jnp.bfloat16),
-            pltpu.VMEM((edge_count, width), jnp.float32),
+            pltpu.VMEM((halo.shape[1], width), jnp.float32),
             pltpu.VMEM((nodes, width), jnp.float32),
             pltpu.SemaphoreType.DMA((devices,)),
             pltpu.SemaphoreType.DMA((devices,)),

time: 130 us -> 127 us (0.977)
  Pallas kernels: 120 us -> 117 us
    pallas_call x1, Pallas kernels: 28.5 us -> 25.4 us  [shards(): pl.pallas_call(functools.partial(processor_kernel, step, faces, subs), ou...]
where the time goes in v1:
time: 127 us; the launch traced here: 126 us
  Pallas kernels  117 us (92%)
  local copies, waits for them, and re-layouts  6.43 us (5%)
  other arithmetic  2.8 us (2%)
    pallas_call x1, Pallas kernels, shards(): pl.pallas_call(functools.partial(embed_kernel, min(64, capacity), subs),...  48.5 us
    pallas_call x1, Pallas kernels, shards(): pl.pallas_call(functools.partial(edge_kernel, min(256, capacity), subs),...  43.2 us
    pallas_call x1, Pallas kernels, shards(): pl.pallas_call(functools.partial(processor_kernel, step, faces, subs), ou...  25.4 us
    unnamed x15, local copies, waits for them, and re-layouts  2.6 us

profile of v1, /device:TPU:0, one launch (start us, length us, event | category | flops | bytes accessed | tf_op | source)
XLA Modules:
  0.0 126.4 jit_solution(16615435482016030822)
XLA Ops:
  0.0 0.0 copy-start.4
  0.0 0.7 fusion
  0.8 0.8 copy.28
  1.6 0.1 pad.17.clone
  1.6 0.7 maximum_bitcast_fusion.aux_ref
  2.4 1.3 %broadcast_maximum_fusion.index_ref = s32[8,512]{1,0:T(8,128)} fusion(s32[8,512]{1,0:T(8,128)} %param.29), kind=kLoop, calls=%fused_computation.5 | loop fusion | flops 4096 | bytes 32768 | tf_op jit(solution)/shard_map/max | solution.py:533
  3.7 48.5 %embed.1 = (f32[8,512,4,128]{3,2,1,0:T(4,128)}, bf16[8,320,512]{2,1,0:T(8,128)(2,1)}, bf16[8,16,512]{2,1,0:T(8,128)(2,1)}) custom-call(s32[8,512]{1,0:T(8,128)} %broadcast_maximum_fusion.index_ref, bf16[474,4096]{1,0:T(8,128)(2,1)} %bitcast.7, bf16[474,512]{1,0:T(8,128)(2,1)} %first_ref.1, bf16[512,512]{1,0:T(8,128)(2,1)} %second_ref.1, ...), custom_call_target="tpu_custom_call" | custom-call | tf_op jit(solution)/shard_map/embed/pallas_call | solution.py:500
  52.3 0.0 copy-done.4
  52.3 0.6 pad.11.feature_ref
  52.9 0.0 copy-start
  52.9 0.0 copy-start.3
  52.9 0.0 copy-start.5
  52.9 0.0 copy-start.1
  52.9 0.0 copy-start.2
  52.9 43.2 %edges.1.sum_ref = bf16[320,512]{1,0:T(8,128)(2,1)} custom-call(f32[8,512,4,128]{3,2,1,0:T(4,128)} %get-tuple-element.8.sent_ref, bf16[8,320,512]{2,1,0:T(8,128)(2,1)} %get-tuple-element.9.nodes_ref, bf16[8,16,512]{2,1,0:T(8,128)(2,1)} %get-tuple-element.10.aux_ref, bf16[512,512]{1,0:T(8,128)(2,1)} %receiver_ref.1, bf16[16,512]{1,0:T(8,128)(2,1)} %pad.11.feature_ref, ...), custom_call_target="tpu_custom_call" | custom-call | tf_op jit(solution)/shard_map/edges/pallas_call | solution.py:545
  96.1 0.0 copy-done
  96.1 0.6 pad.12.edges_ref
  96.7 0.0 copy-done.3
  96.7 0.1 copy.31
  96.8 0.7 reshape.9.halo_ref
  97.5 0.0 copy-done.5
  97.5 0.6 pad.13.feature_ref
  98.1 0.0 copy-done.1
  98.1 0.6 reshape.10.source_ref
  98.7 0.0 copy-done.2
  98.7 0.6 reshape.11.target_ref
  99.3 25.4 %processor.1 = bf16[320,512]{1,0:T(8,128)(2,1)} custom-call(bf16[320,512]{1,0:T(8,128)(2,1)} %nodes_ref.3, bf16[320,512]{1,0:T(8,128)(2,1)} %edges.1.sum_ref, s32[1,512]{1,0:T(1,128)} %reshape.9.halo_ref, s32[1,2560]{1,0:T(1,128)} %reshape.10.source_ref, s32[1,2560]{1,0:T(1,128)} %reshape.11.target_ref, bf16[16,2560]{1,0:T(8,128)(2,1)} %pad.12.edges_ref, ...), custom_call_target="tpu_custom_call" | custom-call | tf_op jit(solution)/shard_map/processor/pallas_call | solution.py:594
  124.7 1.7 %copy.33 = bf16[320,512]{1,0:T(8,128)(2,1)} copy(bf16[320,512]{1,0:T(8,128)(2,1)} %processor.1) | data formatting | bytes 655360
  (3 shorter events, 0.0 us)
Async XLA Ops:
  0.0 52.3 %copy-start.4 = (bf16[4,512]{1,0:T(4,128)(2,1)S(1)}, bf16[4,512]{1,0:T(4,128)(2,1)}, u32[]{:S(2)}) copy-start(bf16[4,512]{1,0:T(4,128)(2,1)} %param.36) | copy-start | bytes 12292
  52.9 43.2 %copy-start = (bf16[4,2560]{1,0:T(4,128)(2,1)S(1)}, bf16[4,2560]{1,0:T(4,128)(2,1)}, u32[]{:S(2)}) copy-start(bf16[4,2560]{1,0:T(4,128)(2,1)} %param.28) | copy-start | bytes 61444
  52.9 43.8 %copy-start.3 = (s32[32,16]{0,1:T(8,128)S(1)}, s32[32,16]{0,1:T(8,128)}, u32[]{:S(2)}) copy-start(s32[32,16]{0,1:T(8,128)} %param.31) | copy-start | bytes 6148
  52.9 44.6 %copy-start.5 = (bf16[4,512]{1,0:T(4,128)(2,1)S(1)}, bf16[4,512]{1,0:T(4,128)(2,1)}, u32[]{:S(2)}) copy-start(bf16[4,512]{1,0:T(4,128)(2,1)} %param.43) | copy-start | bytes 12292
  52.9 45.2 %copy-start.1 = (s32[2560]{0:T(1024)S(1)}, s32[2560]{0:T(1024)}, u32[]{:S(2)}) copy-start(s32[2560]{0:T(1024)} %param.32) | copy-start | bytes 30724
  52.9 45.8 %copy-start.2 = (s32[2560]{0:T(1024)S(1)}, s32[2560]{0:T(1024)}, u32[]{:S(2)}) copy-start(s32[2560]{0:T(1024)} %param.33) | copy-start | bytes 30724

commit v2 on v1

v2 whole, which is shorter than its diff:
```python
import functools

import jax
import jax.numpy as jnp
from jax import lax
from jax.experimental import pallas as pl
from jax.experimental.pallas import tpu as pltpu
from jax.sharding import PartitionSpec as P

EPSILON = 1e-05
LANES = 128
MESH_ID = pl.DeviceIdType.MESH


def silu(values):
    half = values * 0.5
    return (half + half * jnp.tanh(half)).astype(jnp.bfloat16)


def norm(values):
    width = values.shape[-1]
    centered = values - jnp.sum(values, axis=-1, keepdims=True) * (1.0 / width)
    spread = jnp.sum(centered * centered, axis=-1, keepdims=True) * (1.0 / width)
    return centered * lax.rsqrt(spread + EPSILON)


def dot(a, b):
    return jnp.dot(a, b, preferred_element_type=jnp.float32)


def dot_t(a, b):
    return lax.dot_general(a, b, (((0,), (0,)), ((), ())), preferred_element_type=jnp.float32)


def pick(count, index):
    rows = lax.broadcasted_iota(jnp.int32, (count, index.shape[1]), 0)
    return jnp.where(rows == index, 1.0, 0.0).astype(jnp.bfloat16)


def sub_at(position, subs):
    position = lax.rem(position + subs, subs)
    return jnp.where(position < subs // 2, 2 * position, 2 * (subs - 1 - position) + 1)


def ring_position(subs):
    sub = lax.axis_index("sub")
    return jnp.where(lax.rem(sub, 2) == 0, sub // 2, subs - 1 - sub // 2)


def device_at(position, subs):
    return (lax.axis_index("face"), sub_at(position, subs))


def ring_distance(place, subs):
    half = lax.div(place + 1, 2)
    ahead = subs // 2 - half
    return jnp.where(lax.rem(place, 2) == 1, ahead, lax.rem(subs // 2 + half, subs))


def encoder_kernel(
    rows,
    subs,
    index_ref,
    edges_ref,
    receive_ref,
    feature_ref,
    x_hbm,
    nodes_hbm,
    first_hbm,
    second_hbm,
    sender_hbm,
    receiver_hbm,
    output_hbm,
    out_ref,
    x,
    nodes,
    first,
    square,
    load_sem,
    x_sem,
    table,
    picked,
    aux,
    aux_in,
    terms,
    wide_table,
    acc,
    kept,
    outbox,
    inbox,
    side_send,
    side_recv,
    gather_send,
    gather_recv,
    sum_send,
    sum_recv,
):
    count, width = nodes.shape
    feats = edges_ref.shape[0]
    capacity = index_ref.shape[1]
    points = x.shape[1]
    parts = width // LANES
    far = subs // 2
    pieces = 4
    piece = count // pieces
    steps = points // rows
    here = ring_position(subs)

    loads = [
        pltpu.make_async_copy(nodes_hbm, nodes, load_sem.at[0]),
        pltpu.make_async_copy(receiver_hbm, square.at[0], load_sem.at[1]),
        pltpu.make_async_copy(first_hbm, first, load_sem.at[2]),
        pltpu.make_async_copy(second_hbm, square.at[1], load_sem.at[3]),
        pltpu.make_async_copy(sender_hbm, square.at[2], load_sem.at[4]),
        pltpu.make_async_copy(output_hbm, square.at[3], load_sem.at[5]),
    ]

    def load_x(step):
        span = pl.ds(pl.multiple_of(step * rows, rows), rows)
        return pltpu.make_async_copy(x_hbm.at[:, span], x.at[:, span], x_sem.at[step])

    loads[0].start()
    loads[1].start()
    loads[2].start()
    load_x(0).start()
    loads[3].start()
    loads[4].start()

    @pl.loop(1, steps)
    def _(step):
        load_x(step).start()

    loads[5].start()

    barrier = pltpu.get_barrier_semaphore()
    for distance in range(1, subs):
        pl.semaphore_signal(
            barrier, inc=1, device_id=device_at(here + distance, subs), device_id_type=MESH_ID
        )

    received = receive_ref[...]
    high = lax.div(received + 16, 16) - 1
    low = (received - high * 16).astype(jnp.float32)
    high = high.astype(jnp.float32)
    tags = [edges_ref[feat].astype(jnp.float32) for feat in range(feats)]
    fill = jnp.zeros((8 - feats - 2, capacity), jnp.float32)
    for source in range(subs):
        span = slice(source, source + 1)
        block = jnp.concatenate(
            [tag[span, :] for tag in tags] + [high[span, :], low[span, :], fill], axis=0
        )
        aux[source] = jnp.concatenate(
            [block[:, : capacity // 2], block[:, capacity // 2 :]], axis=0
        ).astype(jnp.bfloat16)
    table[0] = jnp.zeros((parts, LANES), jnp.float32)
    wide_table[count:, :] = jnp.zeros((16, width), jnp.bfloat16)
    wide_table[count : count + feats, :] = feature_ref[...]

    loads[0].wait()
    loads[1].wait()
    terms[0] = dot(nodes[...], square[0]).astype(jnp.bfloat16)
    pl.semaphore_wait(barrier, subs - 1)

    def gather(flow, hop, part):
        sign = 1 - 2 * flow
        span = pl.ds((2 * flow + part) * piece, piece)
        return pltpu.make_async_remote_copy(
            src_ref=terms.at[(-sign * hop) % subs, span, :],
            dst_ref=terms.at[(-sign * (hop + 1)) % subs, span, :],
            send_sem=gather_send.at[flow, 2 * hop + part],
            recv_sem=gather_recv.at[flow, 2 * hop + part],
            device_id=device_at(here + sign, subs),
            device_id_type=MESH_ID,
        )

    relays = 2 * (subs - 2)

    def relay(event):
        hop, part = event // 2 + 1, event % 2
        for flow in range(2):
            gather(flow, hop - 1, part).wait_recv()
            gather(flow, hop, part).start()

    def side(distance):
        return pltpu.make_async_remote_copy(
            src_ref=aux.at[sub_at(here + distance, subs)],
            dst_ref=aux_in.at[subs - distance],
            send_sem=side_send.at[distance],
            recv_sem=side_recv.at[distance],
            device_id=device_at(here + distance, subs),
            device_id_type=MESH_ID,
        )

    for part in range(2):
        for flow in range(2):
            gather(flow, 0, part).start()
    for distance in range(1, subs):
        side(distance).start()
    aux_in[0] = aux[sub_at(here, subs)]

    for load in loads[2:5]:
        load.wait()

    done = min(steps - 1, relays)

    @pl.loop(0, steps)
    def _(step):
        load_x(step).wait()
        start = pl.multiple_of(step * rows, rows)
        hidden = silu(dot_t(x[:, pl.ds(start, rows)], first[...]))
        latent = norm(dot(hidden, square[1])).astype(jnp.bfloat16)
        sent = dot(latent, square[2])
        for part in range(parts):
            table[pl.ds(start + 1, rows), part, :] = sent[:, part * LANES : (part + 1) * LANES]
        for event in range(done):

            @pl.when(step == event + 1)
            def _():
                relay(event)

    loads[5].wait()

    def pass_on(flow, stage, part):
        sign = 1 - 2 * flow
        span = pl.ds(part * piece, piece)
        return pltpu.make_async_remote_copy(
            src_ref=outbox.at[flow, stage - 1, span, :],
            dst_ref=inbox.at[flow, stage - 1, span, :],
            send_sem=sum_send.at[flow, stage - 1, part],
            recv_sem=sum_recv.at[flow, stage - 1, part],
            device_id=device_at(here + sign, subs),
            device_id_type=MESH_ID,
        )

    def has(flow, stage, part):
        return stage < far or part // 2 == flow

    def place_of(flow, stage):
        if stage == far:
            return 0
        return 2 * (far - stage) - 1 + flow

    def push(flow, stage, part):
        span = slice(part * piece, (part + 1) * piece)
        value = kept[place_of(flow, stage), span, :]
        if stage < far and has(flow, stage + 1, part):
            pass_on(flow, stage + 1, part).wait_recv()
            value = value.astype(jnp.float32) + inbox[flow, stage, span, :].astype(jnp.float32)
            value = value.astype(jnp.bfloat16)
        outbox[flow, stage - 1, span, :] = value
        pass_on(flow, stage, part).start()

    def push_early(stage):
        for part in range(2):
            for flow in range(2):
                if stage == far:
                    push(flow, stage, 2 * flow + part)
                else:
                    push(flow, stage, 2 * (1 - flow) + part)

    def push_late(stage):
        for part in range(2):
            for flow in range(2):
                push(flow, stage, 2 * flow + part)

    events = {place: [] for place in range(subs)}
    events[0].append(functools.partial(push_early, far))
    for turn in range(1, far):
        early = min(3 * turn - 1, subs - 1)
        late = max(early, min(2 * turn + 2, subs - 1))
        events[early].append(functools.partial(push_early, far - turn))
        events[late].append(functools.partial(push_late, far - turn))
    waits = {point: [] for point in range(2 * subs)}
    for event in range(done, relays):
        turn = event // 2 - far + 1
        point = max(0, turn) if turn < 2 else 4 * turn - 4
        waits[point + event % 2 if turn > 0 else 0].append(functools.partial(relay, event))
    hops = subs - 1

    def arrive(distance):
        for flow in range(2):
            hop = (distance if flow == 1 else subs - distance) - 1
            for part in range(2):
                if hop == hops - 1:
                    gather(flow, hop, part).wait_recv()

    @pl.loop(0, subs)
    def _(place):
        distance = ring_distance(place, subs)
        target = sub_at(here + distance, subs)
        for spot in range(capacity):
            picked[spot] = table[index_ref[target, spot] + 1]
        for when in range(subs):
            if when == 0 or waits[2 * when]:

                @pl.when(place == when)
                def _():
                    if when == 0:
                        for away in range(1, subs):
                            side(away).wait()
                    for action in waits[2 * when]:
                        action()

        @pl.when(place == subs - 3)
        def _():
            arrive(1)
            arrive(subs - 1)

        wide_table[:count, :] = terms[distance]
        halves = aux_in[distance].astype(jnp.float32)
        info = jnp.concatenate([halves[:8, :], halves[8:, :]], axis=1)
        index = (info[feats : feats + 1, :] * 16.0 + info[feats + 1 : feats + 2, :]).astype(
            jnp.int32
        )
        chosen = pick(count, index)
        wide = jnp.concatenate(
            [chosen, jnp.concatenate([info, jnp.zeros_like(info)], axis=0).astype(jnp.bfloat16)],
            axis=0,
        )
        sent = jnp.concatenate([picked[:, part, :] for part in range(parts)], axis=1)
        summed = dot_t(wide, wide_table[...]) + sent
        message = norm(dot(silu(summed), square[3])).astype(jnp.bfloat16)
        acc[...] = dot(chosen, message)
        kept[place] = acc[...].astype(jnp.bfloat16)
        for when in range(subs):

            @pl.when(place == when)
            def _():
                for action in waits[2 * when + 1] + events[when]:
                    action()

    for part in range(pieces):
        span = slice(part * piece, (part + 1) * piece)
        total = acc[span, :]
        for flow in range(2):
            if has(flow, 1, part):
                pass_on(flow, 1, part).wait_recv()
                total = total + inbox[flow, 0, span, :].astype(jnp.float32)
        out_ref[span, :] = total.astype(jnp.bfloat16)
    for flow in range(2):
        for hop in range(hops):
            for part in range(2):
                gather(flow, hop, part).wait_send()
        for stage in range(1, far + 1):
            for part in range(pieces):
                if has(flow, stage, part):
                    pass_on(flow, stage, part).wait_send()


def partner(step, faces, subs):
    face, sub = lax.axis_index("face"), lax.axis_index("sub")
    return flip(face, lax.rem(step, faces), faces), flip(sub, step // faces, subs)


def flip(index, mask, count):
    total, bit = 0, 1
    while bit < count:
        total = total + lax.rem(lax.rem(index // bit, 2) + lax.rem(mask // bit, 2), 2) * bit
        bit *= 2
    return total


def processor_kernel(
    block,
    faces,
    subs,
    nodes_ref,
    sum_ref,
    halo_ref,
    source_ref,
    target_ref,
    edges_ref,
    feature_ref,
    *rest,
):
    weights, rest = rest[:9], rest[9:]
    (
        out_ref,
        held,
        held_sem,
        outgoing,
        arrived,
        local_table,
        base,
        acc,
        send_sem,
        recv_sem,
    ) = rest

    def fetch(place):
        return pltpu.make_async_copy(weights[place], held.at[place], held_sem.at[place])

    for place in range(len(weights)):
        fetch(place).start()

    def weight(place):
        fetch(place).wait()
        return held[place]

    devices = faces * subs
    me = lax.axis_index("face") * subs + lax.axis_index("sub")
    nodes, width = nodes_ref.shape
    slots = halo_ref.shape[1] // devices
    table_slots = devices * slots
    edges = source_ref.shape[1]
    barrier = pltpu.get_barrier_semaphore()

    @pl.loop(1, devices)
    def _(step):
        face, sub = partner(step, faces, subs)
        pl.semaphore_signal(barrier, inc=1, device_id=(face, sub), device_id_type=MESH_ID)

    start = nodes_ref[...]
    before = dot(start, weight(0)) + dot(sum_ref[...], weight(1))
    refined = norm(dot(silu(before), weight(2)))
    state = (start.astype(jnp.float32) + refined).astype(jnp.bfloat16)
    outgoing[...] = dot_t(pick(nodes, halo_ref[...]), state).astype(jnp.bfloat16)
    arrived[pl.ds(pl.multiple_of(me * slots, slots), slots), :] = jnp.zeros(
        (slots, width), jnp.bfloat16
    )
    pl.semaphore_wait(barrier, devices - 1)

    def copy(step):
        face, sub = partner(step, faces, subs)
        other = face * subs + sub
        return pltpu.make_async_remote_copy(
            src_ref=outgoing.at[pl.ds(pl.multiple_of(other * slots, slots), slots), :],
            dst_ref=arrived.at[pl.ds(pl.multiple_of(me * slots, slots), slots), :],
            send_sem=send_sem.at[step],
            recv_sem=recv_sem.at[step],
            device_id=(face, sub),
            device_id_type=MESH_ID,
        )

    @pl.loop(1, devices)
    def _(step):
        copy(devices - step).start()

    local_table[:nodes, :] = dot(state, weight(3)).astype(jnp.bfloat16)
    local_table[nodes : 2 * nodes, :] = dot(state, weight(4)).astype(jnp.bfloat16)
    local_table[2 * nodes :, :] = feature_ref[...]
    own_part = dot(state, weight(6))

    group = min(512, table_slots)
    source = source_ref[...]
    target = target_ref[...]
    tags = edges_ref[...]
    high = (target // 16).astype(jnp.float32)
    low = (target - (target // 16) * 16).astype(jnp.float32)
    digits = jnp.concatenate(
        [high, low, jnp.ones_like(high), jnp.zeros((13, edges), jnp.float32)], axis=0
    ).astype(jnp.bfloat16)
    info = jnp.concatenate([tags, digits], axis=0)
    spots = []
    for first in range(0, table_slots, group):
        rows = lax.broadcasted_iota(jnp.int32, (group, edges), 0) + (nodes + first)
        reads = jnp.where(rows == source, 1.0, 0.0).astype(jnp.bfloat16)
        found = lax.dot_general(
            reads, info, (((1,), (1,)), ((), ())), preferred_element_type=jnp.float32
        )
        spot = found[:, 16:17] * 16.0 + found[:, 17:18] + found[:, 18:19] - 1.0
        spot = spot.astype(jnp.int32)
        lanes = lax.broadcasted_iota(jnp.int32, (group, nodes), 1)
        chosen = jnp.where(lanes == spot, 1.0, 0.0).astype(jnp.bfloat16)
        base[first : first + group, :] = dot(chosen, local_table[nodes : 2 * nodes, :]) + dot(
            found[:, :16].astype(jnp.bfloat16), local_table[2 * nodes :, :]
        )
        spots.append(chosen)

    fetch(5).wait()
    for first in range(0, edges, block):
        span = slice(first, first + block)
        wide = jnp.concatenate(
            [
                pick(nodes, source_ref[:, span]),
                pick(nodes, target_ref[:, span]),
                edges_ref[:, span],
            ],
            axis=0,
        )
        total = dot_t(wide, local_table[...])
        message = norm(dot(silu(total), held[5])).astype(jnp.bfloat16)
        kept = jnp.where(source_ref[:, span] < nodes, target_ref[:, span], -1)
        if first == 0:
            acc[...] = dot(pick(nodes, kept), message)
        else:
            acc[...] += dot(pick(nodes, kept), message)

    @pl.loop(1, devices)
    def _(step):
        copy(devices - step).wait()

    for place, first in enumerate(range(0, table_slots, group)):
        span = slice(first, first + group)
        total = base[span, :] + dot(arrived[span, :], held[3])
        message = norm(dot(silu(total), held[5])).astype(jnp.bfloat16)
        acc[...] += dot_t(spots[place], message)
    after = own_part + dot(acc[...].astype(jnp.bfloat16), weight(7))
    final = norm(dot(silu(after), weight(8)))
    out_ref[...] = (state.astype(jnp.float32) + final).astype(jnp.bfloat16)


def vmem():
    return pl.BlockSpec(memory_space=pltpu.VMEM)


def smem():
    return pl.BlockSpec(memory_space=pltpu.SMEM)


def shards(
    grid_inputs,
    mesh_nodes,
    encoder_edges,
    mesh_edges,
    grid_send,
    node_receive,
    halo_send,
    edge_source,
    edge_target,
    embed_first,
    embed_second,
    encoder_feature,
    encoder_sender,
    encoder_receiver,
    encoder_output,
    updater_self,
    updater_message,
    updater_output,
    processor_feature,
    processor_sender,
    processor_receiver,
    processor_output,
    refiner_self,
    refiner_message,
    refiner_output,
):
    subs = lax.axis_size("sub")
    faces = lax.axis_size("face")
    devices = subs * faces
    grid_rows, inputs = grid_inputs.shape
    nodes, width = mesh_nodes.shape
    capacity = grid_send.shape[1]
    parts = width // LANES
    feats = encoder_edges.shape[0]

    anywhere = pl.BlockSpec(memory_space=pl.ANY)
    rows = min(512, grid_rows)
    pieces, far = 4, subs // 2
    summed = pl.pallas_call(
        functools.partial(encoder_kernel, rows, subs),
        out_shape=jax.ShapeDtypeStruct((nodes, width), jnp.bfloat16),
        in_specs=[smem(), vmem(), vmem(), vmem()] + [anywhere] * 7,
        out_specs=vmem(),
        scratch_shapes=[
            pltpu.VMEM((inputs, grid_rows), jnp.bfloat16),
            pltpu.VMEM((nodes, width), jnp.bfloat16),
            pltpu.VMEM((inputs, width), jnp.bfloat16),
            pltpu.VMEM((4, width, width), jnp.bfloat16),
            pltpu.SemaphoreType.DMA((6,)),
            pltpu.SemaphoreType.DMA((grid_rows // rows,)),
            pltpu.VMEM((grid_rows + 1, parts, LANES), jnp.float32),
            pltpu.VMEM((capacity, parts, LANES), jnp.float32),
            pltpu.VMEM((subs, 16, capacity // 2), jnp.bfloat16),
            pltpu.VMEM((subs, 16, capacity // 2), jnp.bfloat16),
            pltpu.VMEM((subs, nodes, width), jnp.bfloat16),
            pltpu.VMEM((nodes + 16, width), jnp.bfloat16),
            pltpu.VMEM((nodes, width), jnp.float32),
            pltpu.VMEM((subs, nodes, width), jnp.bfloat16),
            pltpu.VMEM((2, far, nodes, width), jnp.bfloat16),
            pltpu.VMEM((2, far, nodes, width), jnp.bfloat16),
            pltpu.SemaphoreType.DMA((subs,)),
            pltpu.SemaphoreType.DMA((subs,)),
            pltpu.SemaphoreType.DMA((2, 2 * (subs - 1))),
            pltpu.SemaphoreType.DMA((2, 2 * (subs - 1))),
            pltpu.SemaphoreType.DMA((2, far, pieces)),
            pltpu.SemaphoreType.DMA((2, far, pieces)),
        ],
        compiler_params=pltpu.CompilerParams(
            collective_id=1, has_side_effects=True, vmem_limit_bytes=60 * 2**20
        ),
        name="encoder",
    )(
        grid_send,
        encoder_edges,
        node_receive,
        encoder_feature,
        grid_inputs.T,
        mesh_nodes,
        embed_first,
        embed_second,
        encoder_sender,
        encoder_receiver,
        encoder_output,
    )

    pad_feature = lambda weight: jnp.pad(weight, ((0, 16 - feats), (0, 0)))
    edge_count = edge_source.shape[0]
    halo = halo_send.reshape(1, -1)
    step = min(512, edge_count)
    operands = (
        mesh_nodes,
        summed,
        halo,
        edge_source.reshape(1, -1),
        edge_target.reshape(1, -1),
        jnp.pad(mesh_edges, ((0, 16 - feats), (0, 0))),
        pad_feature(processor_feature),
        updater_self,
        updater_message,
        updater_output,
        processor_sender,
        processor_receiver,
        processor_output,
        refiner_self,
        refiner_message,
        refiner_output,
    )
    return pl.pallas_call(
        functools.partial(processor_kernel, step, faces, subs),
        out_shape=jax.ShapeDtypeStruct((nodes, width), jnp.bfloat16),
        in_specs=[vmem()] * (len(operands) - 9) + [anywhere] * 9,
        out_specs=vmem(),
        scratch_shapes=[
            pltpu.VMEM((9, width, width), jnp.bfloat16),
            pltpu.SemaphoreType.DMA((9,)),
            pltpu.VMEM((halo.shape[1], width), jnp.bfloat16),
            pltpu.VMEM((halo.shape[1], width), jnp.bfloat16),
            pltpu.VMEM((2 * nodes + 16, width), jnp.bfloat16),
            pltpu.VMEM((halo.shape[1], width), jnp.float32),
            pltpu.VMEM((nodes, width), jnp.float32),
            pltpu.SemaphoreType.DMA((devices,)),
            pltpu.SemaphoreType.DMA((devices,)),
        ],
        compiler_params=pltpu.CompilerParams(
            collective_id=0, has_side_effects=True, vmem_limit_bytes=60 * 2**20
        ),
        name="processor",
    )(*operands)


def solution(mesh):
    rows = P(("face", "sub"), None)
    placed = (
        rows,
        rows,
        P(None, ("face", "sub"), None),
        P(None, ("face", "sub")),
        rows,
        rows,
        rows,
        P(("face", "sub")),
        P(("face", "sub")),
    ) + (P(),) * 16
    return jax.shard_map(
        shards, mesh=mesh, in_specs=placed, out_specs=P(("face", "sub"), None), check_vma=False
    )
```

time: 127 us -> 94.9 us (0.75)
  Pallas kernels: 117 us -> 85.9 us
  other arithmetic: 2.8 us -> 0 us
  local copies, waits for them, and re-layouts: 6.43 us -> 8.43 us
    pallas_call x2 -> x1, Pallas kernels: 91.7 us -> 62.3 us  [shards(): pl.pallas_call(functools.partial(encoder_kernel, rows, subs), out_shape=j...]
    pallas_call x1, Pallas kernels: 25.4 us -> 23.6 us  [shards(): pl.pallas_call(functools.partial(processor_kernel, step, faces, subs), ou...]
    max x1 -> x0, other arithmetic: 1.32 us -> none  [shards(): jnp.maximum(grid_send, 0)]
    unnamed x15 -> x2, local copies, waits for them, and re-layouts: 2.6 us -> 2.49 us
where the time goes in v2:
time: 94.9 us; the launch traced here: 94.4 us
  Pallas kernels  85.9 us (91%)
  local copies, waits for them, and re-layouts  8.43 us (9%)
    pallas_call x1, Pallas kernels, shards(): pl.pallas_call(functools.partial(encoder_kernel, rows, subs), out_shape=j...  62.3 us
    pallas_call x1, Pallas kernels, shards(): pl.pallas_call(functools.partial(processor_kernel, step, faces, subs), ou...  23.6 us
    unnamed x2, local copies, waits for them, and re-layouts  2.49 us

profile of v2, /device:TPU:0, one launch (start us, length us, event | category | flops | bytes accessed | tf_op | source)
XLA Modules:
  0.0 94.4 jit_solution(1726959980623691023)
XLA Ops:
  0.0 1.3 %reshape.10.source_ref = s32[1,2560]{1,0:T(1,128)} reshape(s32[2560]{0:T(1024)} %param.32) | data formatting | bytes 20480 | tf_op jit(solution)/shard_map/reshape | solution.py:605
  1.3 1.3 %reshape.11.target_ref = s32[1,2560]{1,0:T(1,128)} reshape(s32[2560]{0:T(1024)} %param.33) | data formatting | bytes 20480 | tf_op jit(solution)/shard_map/reshape | solution.py:606
  2.6 0.8 copy.27
  3.4 0.7 reshape.9.halo_ref
  4.1 1.3 %pad.9.feature_ref = bf16[16,512]{1,0:T(8,128)(2,1)} pad(bf16[4,512]{1,0:T(4,128)(2,1)} %param.43, bf16[]{:T(256)} %constant.2.clone.1), padding=0_12x0_0 | pad | bytes 20482 | tf_op jit(solution)/shard_map/jit(_pad)/pad | solution.py:597
  5.3 1.4 %pad.8.edges_ref = bf16[16,2560]{1,0:T(8,128)(2,1)} pad(bf16[4,2560]{1,0:T(4,128)(2,1)} %param.28, bf16[]{:T(256)} %constant.2.clone.1), padding=0_12x0_0 | pad | bytes 102402 | tf_op jit(solution)/shard_map/jit(_pad)/pad | solution.py:607
  6.7 62.3 %encoder.1.sum_ref = bf16[320,512]{1,0:T(8,128)(2,1)} custom-call(s32[8,512]{1,0:T(8,128)} %index_ref.1, bf16[4,8,512]{2,1,0:T(8,128)(2,1)} %edges_ref.1, s32[8,512]{1,0:T(8,128)} %receive_ref.1, bf16[4,512]{1,0:T(4,128)(2,1)} %feature_ref.1, bf16[474,4096]{1,0:T(8,128)(2,1)} %bitcast.1, bf16[320,512]{1,0:T(8,128)(2,1)} %nodes_ref.1, ...), custom_call_target="tpu_custom_call" | custom-call | tf_op jit(solution)/shard_map/encoder/pallas_call | solution.py:550
  69.0 23.6 %processor.1 = bf16[320,512]{1,0:T(8,128)(2,1)} custom-call(bf16[320,512]{1,0:T(8,128)(2,1)} %nodes_ref.1, bf16[320,512]{1,0:T(8,128)(2,1)} %encoder.1.sum_ref, s32[1,512]{1,0:T(1,128)} %reshape.9.halo_ref, s32[1,2560]{1,0:T(1,128)} %reshape.10.source_ref, s32[1,2560]{1,0:T(1,128)} %reshape.11.target_ref, bf16[16,2560]{1,0:T(8,128)(2,1)} %pad.8.edges_ref, ...), custom_call_target="tpu_custom_call" | custom-call | tf_op jit(solution)/shard_map/processor/pallas_call | solution.py:619
  92.7 1.7 %copy.29 = bf16[320,512]{1,0:T(8,128)(2,1)} copy(bf16[320,512]{1,0:T(8,128)(2,1)} %processor.1) | data formatting | bytes 655360

commit v3 on v2

v3 whole, which is shorter than its diff:
```python
import functools

import jax
import jax.numpy as jnp
from jax import lax
from jax.experimental import pallas as pl
from jax.experimental.pallas import tpu as pltpu
from jax.sharding import PartitionSpec as P

EPSILON = 1e-05
LANES = 128
MESH_ID = pl.DeviceIdType.MESH


def silu(values):
    half = values * 0.5
    return (half + half * jnp.tanh(half)).astype(jnp.bfloat16)


def norm(values):
    width = values.shape[-1]
    centered = values - jnp.sum(values, axis=-1, keepdims=True) * (1.0 / width)
    spread = jnp.sum(centered * centered, axis=-1, keepdims=True) * (1.0 / width)
    return centered * lax.rsqrt(spread + EPSILON)


def dot(a, b):
    return jnp.dot(a, b, preferred_element_type=jnp.float32)


def dot_t(a, b):
    return lax.dot_general(a, b, (((0,), (0,)), ((), ())), preferred_element_type=jnp.float32)


def pick(count, index):
    rows = lax.broadcasted_iota(jnp.int32, (count, index.shape[1]), 0)
    return jnp.where(rows == index, 1.0, 0.0).astype(jnp.bfloat16)


def sub_at(position, subs):
    position = lax.rem(position + subs, subs)
    return jnp.where(position < subs // 2, 2 * position, 2 * (subs - 1 - position) + 1)


def ring_position(subs):
    sub = lax.axis_index("sub")
    return jnp.where(lax.rem(sub, 2) == 0, sub // 2, subs - 1 - sub // 2)


def device_at(position, subs):
    return (lax.axis_index("face"), sub_at(position, subs))


def ring_distance(place, subs):
    half = lax.div(place + 1, 2)
    ahead = subs // 2 - half
    return jnp.where(lax.rem(place, 2) == 1, ahead, lax.rem(subs // 2 + half, subs))


def flip(index, mask, count):
    total, bit = 0, 1
    while bit < count:
        total = total + lax.rem(lax.rem(index // bit, 2) + lax.rem(mask // bit, 2), 2) * bit
        bit *= 2
    return total


def partner(step, faces, subs):
    face, sub = lax.axis_index("face"), lax.axis_index("sub")
    return flip(face, lax.rem(step, faces), faces), flip(sub, step // faces, subs)


def digits(values):
    high = lax.div(values + 16, 16) - 1
    low = values - high * 16
    return high.astype(jnp.float32), low.astype(jnp.float32)


def hot(index, count):
    lanes = lax.broadcasted_iota(jnp.int32, (index.shape[0], count), 1)
    return jnp.where(lanes == index, 1.0, 0.0).astype(jnp.bfloat16)


def dot_n(a, b):
    return lax.dot_general(a, b, (((1,), (1,)), ((), ())), preferred_element_type=jnp.float32)


def step_kernel(
    rows,
    block,
    faces,
    subs,
    index_ref,
    edges_ref,
    receive_ref,
    feature_ref,
    halo_ref,
    source_ref,
    target_ref,
    tags_ref,
    tag_feature_ref,
    x_hbm,
    nodes_hbm,
    first_hbm,
    second_hbm,
    sender_hbm,
    receiver_hbm,
    output_hbm,
    *rest,
):
    weights, rest = rest[:9], rest[9:]
    (
        out_ref,
        x,
        nodes,
        first,
        square,
        load_sem,
        x_sem,
        held,
        held_sem,
        table,
        picked,
        aux,
        aux_in,
        terms,
        wide_table,
        acc,
        kept,
        outbox,
        inbox,
        source,
        target,
        tags,
        before,
        leaving,
        spots,
        found,
        outgoing,
        arrived,
        base,
        local_table,
        side_send,
        side_recv,
        gather_send,
        gather_recv,
        sum_send,
        sum_recv,
        halo_send,
        halo_recv,
    ) = rest
    count, width = nodes.shape
    feats = edges_ref.shape[0]
    capacity = index_ref.shape[1]
    points = x.shape[1]
    parts = width // LANES
    far = subs // 2
    pieces = 4
    piece = count // pieces
    steps = points // rows
    here = ring_position(subs)
    barrier = pltpu.get_barrier_semaphore()

    @pl.loop(1, faces * subs)
    def _(step):
        pl.semaphore_signal(
            barrier, inc=1, device_id=partner(step, faces, subs), device_id_type=MESH_ID
        )

    devices = faces * subs
    me = lax.axis_index("face") * subs + lax.axis_index("sub")

    loads = [
        pltpu.make_async_copy(nodes_hbm, nodes, load_sem.at[0]),
        pltpu.make_async_copy(receiver_hbm, square.at[0], load_sem.at[1]),
        pltpu.make_async_copy(first_hbm, first, load_sem.at[2]),
        pltpu.make_async_copy(second_hbm, square.at[1], load_sem.at[3]),
        pltpu.make_async_copy(sender_hbm, square.at[2], load_sem.at[4]),
        pltpu.make_async_copy(output_hbm, square.at[3], load_sem.at[5]),
    ]

    def load_x(step):
        span = pl.ds(pl.multiple_of(step * rows, rows), rows)
        return pltpu.make_async_copy(x_hbm.at[:, span], x.at[:, span], x_sem.at[step])

    loads[0].start()
    loads[1].start()
    loads[2].start()
    load_x(0).start()
    loads[3].start()
    loads[4].start()

    @pl.loop(1, steps)
    def _(step):
        load_x(step).start()

    loads[5].start()

    def fetch(place):
        return pltpu.make_async_copy(weights[place], held.at[place], held_sem.at[place])

    def weight(place):
        fetch(place).wait()
        return held[place]

    for place in range(len(weights)):
        fetch(place).start()

    high, low = digits(receive_ref[...])
    features = [edges_ref[feat].astype(jnp.float32) for feat in range(feats)]
    fill = jnp.zeros((8 - feats - 2, capacity), jnp.float32)
    for sub in range(subs):
        span = slice(sub, sub + 1)
        stack = jnp.concatenate(
            [feature[span, :] for feature in features] + [high[span, :], low[span, :], fill], axis=0
        )
        aux[sub] = jnp.concatenate(
            [stack[:, : capacity // 2], stack[:, capacity // 2 :]], axis=0
        ).astype(jnp.bfloat16)
    table[0] = jnp.zeros((parts, LANES), jnp.float32)
    wide_table[count:, :] = jnp.zeros((16, width), jnp.bfloat16)
    wide_table[count : count + feats, :] = feature_ref[...]

    loads[0].wait()
    loads[1].wait()
    terms[0] = dot(nodes[...], square[0]).astype(jnp.bfloat16)
    pl.semaphore_wait(barrier, devices - 1)

    def gather(flow, hop, part):
        sign = 1 - 2 * flow
        span = pl.ds((2 * flow + part) * piece, piece)
        return pltpu.make_async_remote_copy(
            src_ref=terms.at[(-sign * hop) % subs, span, :],
            dst_ref=terms.at[(-sign * (hop + 1)) % subs, span, :],
            send_sem=gather_send.at[flow, 2 * hop + part],
            recv_sem=gather_recv.at[flow, 2 * hop + part],
            device_id=device_at(here + sign, subs),
            device_id_type=MESH_ID,
        )

    relays = 2 * (subs - 2)

    def relay(event):
        hop, part = event // 2 + 1, event % 2
        for flow in range(2):
            gather(flow, hop - 1, part).wait_recv()
            gather(flow, hop, part).start()

    def side(distance):
        return pltpu.make_async_remote_copy(
            src_ref=aux.at[sub_at(here + distance, subs)],
            dst_ref=aux_in.at[subs - distance],
            send_sem=side_send.at[distance],
            recv_sem=side_recv.at[distance],
            device_id=device_at(here + distance, subs),
            device_id_type=MESH_ID,
        )

    for part in range(2):
        for flow in range(2):
            gather(flow, 0, part).start()
    for distance in range(1, subs):
        side(distance).start()
    aux_in[0] = aux[sub_at(here, subs)]

    for load in loads[2:5]:
        load.wait()

    done = min(steps - 1, relays)

    @pl.loop(0, steps)
    def _(step):
        load_x(step).wait()
        start = pl.multiple_of(step * rows, rows)
        hidden = silu(dot_t(x[:, pl.ds(start, rows)], first[...]))
        latent = norm(dot(hidden, square[1])).astype(jnp.bfloat16)
        sent = dot(latent, square[2])
        for part in range(parts):
            table[pl.ds(start + 1, rows), part, :] = sent[:, part * LANES : (part + 1) * LANES]
        for event in range(done):

            @pl.when(step == event + 1)
            def _():
                relay(event)

    loads[5].wait()

    def pass_on(flow, stage, part):
        sign = 1 - 2 * flow
        span = pl.ds(part * piece, piece)
        return pltpu.make_async_remote_copy(
            src_ref=outbox.at[flow, stage - 1, span, :],
            dst_ref=inbox.at[flow, stage - 1, span, :],
            send_sem=sum_send.at[flow, stage - 1, part],
            recv_sem=sum_recv.at[flow, stage - 1, part],
            device_id=device_at(here + sign, subs),
            device_id_type=MESH_ID,
        )

    def has(flow, stage, part):
        return stage < far or part // 2 == flow

    def place_of(flow, stage):
        if stage == far:
            return 0
        return 2 * (far - stage) - 1 + flow

    def push(flow, stage, part):
        span = slice(part * piece, (part + 1) * piece)
        value = kept[place_of(flow, stage), span, :]
        if stage < far and has(flow, stage + 1, part):
            pass_on(flow, stage + 1, part).wait_recv()
            value = value.astype(jnp.float32) + inbox[flow, stage, span, :].astype(jnp.float32)
            value = value.astype(jnp.bfloat16)
        outbox[flow, stage - 1, span, :] = value
        pass_on(flow, stage, part).start()

    def push_early(stage):
        for part in range(2):
            for flow in range(2):
                if stage == far:
                    push(flow, stage, 2 * flow + part)
                else:
                    push(flow, stage, 2 * (1 - flow) + part)

    def push_late(stage):
        for part in range(2):
            for flow in range(2):
                push(flow, stage, 2 * flow + part)

    events = {place: [] for place in range(subs)}
    events[0].append(functools.partial(push_early, far))
    for turn in range(1, far - 1):
        early = min(3 * turn - 1, subs - 1)
        late = max(early, min(2 * turn + 2, subs - 1))
        events[early].append(functools.partial(push_early, far - turn))
        events[late].append(functools.partial(push_late, far - turn))
    waits = {point: [] for point in range(2 * subs)}
    for event in range(done, relays):
        turn = event // 2 - far + 1
        point = max(0, turn) if turn < 2 else 4 * turn - 4
        waits[point + event % 2 if turn > 0 else 0].append(functools.partial(relay, event))
    hops = subs - 1

    def arrive(distance):
        for flow in range(2):
            hop = (distance if flow == 1 else subs - distance) - 1
            for part in range(2):
                if hop == hops - 1:
                    gather(flow, hop, part).wait_recv()

    @pl.loop(0, subs)
    def _(place):
        distance = ring_distance(place, subs)
        sub = sub_at(here + distance, subs)
        for spot in range(capacity):
            picked[spot] = table[index_ref[sub, spot] + 1]
        for when in range(subs):
            if when == 0 or waits[2 * when]:

                @pl.when(place == when)
                def _():
                    if when == 0:
                        for away in range(1, subs):
                            side(away).wait()
                    for action in waits[2 * when]:
                        action()

        @pl.when(place == subs - 3)
        def _():
            arrive(1)
            arrive(subs - 1)

        wide_table[:count, :] = terms[distance]
        halves = aux_in[distance].astype(jnp.float32)
        info = jnp.concatenate([halves[:8, :], halves[8:, :]], axis=1)
        index = (info[feats : feats + 1, :] * 16.0 + info[feats + 1 : feats + 2, :]).astype(
            jnp.int32
        )
        chosen = pick(count, index)
        wide = jnp.concatenate(
            [chosen, jnp.concatenate([info, jnp.zeros_like(info)], axis=0).astype(jnp.bfloat16)],
            axis=0,
        )
        sent = jnp.concatenate([picked[:, part, :] for part in range(parts)], axis=1)
        summed = dot_t(wide, wide_table[...]) + sent
        message = norm(dot(silu(summed), square[3])).astype(jnp.bfloat16)
        acc[...] = dot(chosen, message)
        kept[place] = acc[...].astype(jnp.bfloat16)
        for when in range(subs):

            @pl.when(place == when)
            def _():
                for action in waits[2 * when + 1] + events[when]:
                    action()

    edges = target_ref.shape[0] * LANES
    slots, table_slots = halo_ref.shape[0], halo_ref.shape[0] * devices
    group = min(512, table_slots)
    for row in range(target_ref.shape[0]):
        span = slice(row * LANES, (row + 1) * LANES)
        source[:, span] = source_ref[row : row + 1, :]
        target[:, span] = target_ref[row : row + 1, :]
    tags[...] = jnp.zeros_like(tags)
    tags[:feats, :] = tags_ref[...]
    before[...] = dot(nodes[...], weight(0))
    high, low = digits(halo_ref[...])
    for start in range(0, table_slots, group):
        spot = lax.broadcasted_iota(jnp.int32, (group, devices), 0) + start
        peer = lax.broadcasted_iota(jnp.int32, (group, devices), 1)
        of_peer = jnp.where(lax.div(spot, slots) == peer, 1.0, 0.0).astype(jnp.bfloat16)
        lists = dot_n(of_peer, high.astype(jnp.bfloat16)) * 16.0
        lists = lists + dot_n(of_peer, low.astype(jnp.bfloat16))
        spot = lax.broadcasted_iota(jnp.int32, (group, slots), 0) + start
        place = lax.broadcasted_iota(jnp.int32, (group, slots), 1)
        index = jnp.sum(
            jnp.where(lax.rem(spot, slots) == place, lists, 0.0), axis=1, keepdims=True
        )
        leaving[start : start + group, :] = hot(index.astype(jnp.int32), count)
    arrived[pl.ds(pl.multiple_of(me * slots, slots), slots), :] = jnp.zeros(
        (slots, width), jnp.bfloat16
    )
    push_early(1)

    high, low = digits(target[...])
    info = jnp.concatenate(
        [
            tags[...],
            jnp.concatenate(
                [high, low, jnp.ones_like(high), jnp.zeros((13, edges), jnp.float32)], axis=0
            ).astype(jnp.bfloat16),
        ],
        axis=0,
    )
    for start in range(0, table_slots, group):
        span = slice(start, start + group)
        spot = lax.broadcasted_iota(jnp.int32, (group, edges), 0) + (count + start)
        reads = jnp.where(spot == source[...], 1.0, 0.0).astype(jnp.bfloat16)
        read = dot_n(reads, info)
        index = read[:, 16:17] * 16.0 + read[:, 17:18] + read[:, 18:19] - 1.0
        chosen = hot(index.astype(jnp.int32), count)
        found[span, :] = jnp.concatenate([chosen, read[:, :16].astype(jnp.bfloat16)], axis=1)
        spots[:, span] = chosen.T
    push_late(1)
    local_table[2 * count :, :] = jnp.zeros((16, width), jnp.bfloat16)
    local_table[2 * count : 2 * count + feats, :] = tag_feature_ref[...]

    totals = []
    for part in range(pieces):
        span = slice(part * piece, (part + 1) * piece)
        total = acc[span, :]
        for flow in range(2):
            if has(flow, 1, part):
                pass_on(flow, 1, part).wait_recv()
                total = total + inbox[flow, 0, span, :].astype(jnp.float32)
        totals.append(total.astype(jnp.bfloat16))
    total = before[...] + dot(jnp.concatenate(totals, axis=0), weight(1))
    refined = norm(dot(silu(total), weight(2)))
    state = (nodes[...].astype(jnp.float32) + refined).astype(jnp.bfloat16)
    for start in range(0, table_slots, group):
        span = slice(start, start + group)
        outgoing[span, :] = dot(leaving[span, :], state).astype(jnp.bfloat16)

    def copy(step):
        face, sub = partner(step, faces, subs)
        other = face * subs + sub
        return pltpu.make_async_remote_copy(
            src_ref=outgoing.at[pl.ds(pl.multiple_of(other * slots, slots), slots), :],
            dst_ref=arrived.at[pl.ds(pl.multiple_of(me * slots, slots), slots), :],
            send_sem=halo_send.at[step],
            recv_sem=halo_recv.at[step],
            device_id=(face, sub),
            device_id_type=MESH_ID,
        )

    @pl.loop(1, devices)
    def _(step):
        copy(devices - step).start()

    local_table[:count, :] = dot(state, weight(3)).astype(jnp.bfloat16)
    local_table[count : 2 * count, :] = dot(state, weight(4)).astype(jnp.bfloat16)
    own_part = dot(state, weight(6))
    for start in range(0, table_slots, group):
        span = slice(start, start + group)
        base[span, :] = dot(found[span, :], local_table[count:, :])
    fetch(5).wait()
    for start in range(0, edges, block):
        span = slice(start, start + block)
        senders, receivers = source[:, span], target[:, span]
        wide = jnp.concatenate(
            [pick(count, senders), pick(count, receivers), tags[:, span]], axis=0
        )
        message = norm(dot(silu(dot_t(wide, local_table[...])), held[5])).astype(jnp.bfloat16)
        chosen = pick(count, jnp.where(senders < count, receivers, -1))
        if start == 0:
            acc[...] = dot(chosen, message)
        else:
            acc[...] += dot(chosen, message)
    for flow in range(2):
        for hop in range(hops):
            for part in range(2):
                gather(flow, hop, part).wait_send()
        for stage in range(1, far + 1):
            for part in range(pieces):
                if has(flow, stage, part):
                    pass_on(flow, stage, part).wait_send()
    fetch(7).wait()
    fetch(8).wait()

    @pl.loop(1, devices)
    def _(step):
        copy(devices - step).wait()

    for start in range(0, table_slots, group):
        span = slice(start, start + group)
        total = base[span, :] + dot(arrived[span, :], held[3])
        message = norm(dot(silu(total), held[5])).astype(jnp.bfloat16)
        acc[...] += dot(spots[:, span], message)
    after = own_part + dot(acc[...].astype(jnp.bfloat16), held[7])
    final = norm(dot(silu(after), held[8]))
    out_ref[...] = (state.astype(jnp.float32) + final).astype(jnp.bfloat16)


def vmem():
    return pl.BlockSpec(memory_space=pltpu.VMEM)


def smem():
    return pl.BlockSpec(memory_space=pltpu.SMEM)


def shards(
    grid_inputs,
    mesh_nodes,
    encoder_edges,
    mesh_edges,
    grid_send,
    node_receive,
    halo_send,
    edge_source,
    edge_target,
    embed_first,
    embed_second,
    encoder_feature,
    encoder_sender,
    encoder_receiver,
    encoder_output,
    updater_self,
    updater_message,
    updater_output,
    processor_feature,
    processor_sender,
    processor_receiver,
    processor_output,
    refiner_self,
    refiner_message,
    refiner_output,
):
    subs = lax.axis_size("sub")
    faces = lax.axis_size("face")
    devices = subs * faces
    grid_rows, inputs = grid_inputs.shape
    nodes, width = mesh_nodes.shape
    capacity = grid_send.shape[1]
    parts = width // LANES
    feats = encoder_edges.shape[0]

    anywhere = pl.BlockSpec(memory_space=pl.ANY)
    rows = min(512, grid_rows)
    pieces, far = 4, subs // 2
    edge_count = edge_source.shape[0]
    table_slots = devices * halo_send.shape[1]
    bf16, f32 = jnp.bfloat16, jnp.float32
    return pl.pallas_call(
        functools.partial(step_kernel, rows, min(512, edge_count), faces, subs),
        out_shape=jax.ShapeDtypeStruct((nodes, width), bf16),
        in_specs=[smem()] + [vmem()] * 8 + [anywhere] * 16,
        out_specs=vmem(),
        scratch_shapes=[
            pltpu.VMEM((inputs, grid_rows), bf16),
            pltpu.VMEM((nodes, width), bf16),
            pltpu.VMEM((inputs, width), bf16),
            pltpu.VMEM((4, width, width), bf16),
            pltpu.SemaphoreType.DMA((6,)),
            pltpu.SemaphoreType.DMA((grid_rows // rows,)),
            pltpu.VMEM((9, width, width), bf16),
            pltpu.SemaphoreType.DMA((9,)),
            pltpu.VMEM((grid_rows + 1, parts, LANES), f32),
            pltpu.VMEM((capacity, parts, LANES), f32),
            pltpu.VMEM((subs, 16, capacity // 2), bf16),
            pltpu.VMEM((subs, 16, capacity // 2), bf16),
            pltpu.VMEM((subs, nodes, width), bf16),
            pltpu.VMEM((nodes + 16, width), bf16),
            pltpu.VMEM((nodes, width), f32),
            pltpu.VMEM((subs, nodes, width), bf16),
            pltpu.VMEM((2, far, nodes, width), bf16),
            pltpu.VMEM((2, far, nodes, width), bf16),
            pltpu.VMEM((1, edge_count), jnp.int32),
            pltpu.VMEM((1, edge_count), jnp.int32),
            pltpu.VMEM((16, edge_count), bf16),
            pltpu.VMEM((nodes, width), f32),
            pltpu.VMEM((table_slots, nodes), bf16),
            pltpu.VMEM((nodes, table_slots), bf16),
            pltpu.VMEM((table_slots, nodes + 16), bf16),
            pltpu.VMEM((table_slots, width), bf16),
            pltpu.VMEM((table_slots, width), bf16),
            pltpu.VMEM((table_slots, width), f32),
            pltpu.VMEM((2 * nodes + 16, width), bf16),
            pltpu.SemaphoreType.DMA((subs,)),
            pltpu.SemaphoreType.DMA((subs,)),
            pltpu.SemaphoreType.DMA((2, 2 * (subs - 1))),
            pltpu.SemaphoreType.DMA((2, 2 * (subs - 1))),
            pltpu.SemaphoreType.DMA((2, far, pieces)),
            pltpu.SemaphoreType.DMA((2, far, pieces)),
            pltpu.SemaphoreType.DMA((devices,)),
            pltpu.SemaphoreType.DMA((devices,)),
        ],
        compiler_params=pltpu.CompilerParams(
            collective_id=1, has_side_effects=True, vmem_limit_bytes=63 * 2**20
        ),
        name="step",
    )(
        grid_send,
        encoder_edges,
        node_receive,
        encoder_feature,
        halo_send.T,
        edge_source.reshape(-1, LANES),
        edge_target.reshape(-1, LANES),
        mesh_edges,
        processor_feature,
        grid_inputs.T,
        mesh_nodes,
        embed_first,
        embed_second,
        encoder_sender,
        encoder_receiver,
        encoder_output,
        updater_self,
        updater_message,
        updater_output,
        processor_sender,
        processor_receiver,
        processor_output,
        refiner_self,
        refiner_message,
        refiner_output,
    )


def solution(mesh):
    rows = P(("face", "sub"), None)
    placed = (
        rows,
        rows,
        P(None, ("face", "sub"), None),
        P(None, ("face", "sub")),
        rows,
        rows,
        rows,
        P(("face", "sub")),
        P(("face", "sub")),
    ) + (P(),) * 16
    return jax.shard_map(
        shards, mesh=mesh, in_specs=placed, out_specs=P(("face", "sub"), None), check_vma=False
    )
```

time: 94.9 us -> 83.4 us (0.88)
  local copies, waits for them, and re-layouts: 8.43 us -> 1.72 us
  Pallas kernels: 85.9 us -> 81.4 us
    pallas_call x2 -> x1, Pallas kernels: 85.9 us -> 81.4 us  [shards(): pl.pallas_call(functools.partial(step_kernel, rows, min(512, edge_count),...]
    reshape x3 -> x0, local copies, waits for them, and re-layouts: 3.28 us -> none  [the longest x1 1.31 us: shards(): edge_source.reshape(1, -1)]
    pad x2 -> x0, local copies, waits for them, and re-layouts: 2.66 us -> none  [the longest x1 1.37 us: shards(): jnp.pad(mesh_edges, ((0, 16 - feats), (0, 0)))]
    unnamed x2 -> x1, local copies, waits for them, and re-layouts: 2.49 us -> 1.72 us
where the time goes in v3:
time: 83.4 us; the launch traced here: 83.2 us
  Pallas kernels  81.4 us (98%)
  local copies, waits for them, and re-layouts  1.72 us (2%)
    pallas_call x1, Pallas kernels, shards(): pl.pallas_call(functools.partial(step_kernel, rows, min(512, edge_count),...  81.4 us
    unnamed x1, local copies, waits for them, and re-layouts  1.72 us

profile of v3, /device:TPU:0, one launch (start us, length us, event | category | flops | bytes accessed | tf_op | source)
XLA Modules:
  0.0 83.2 jit_solution(14879887222703833899)
XLA Ops:
  0.0 81.4 %step.1 = bf16[320,512]{1,0:T(8,128)(2,1)} custom-call(s32[8,512]{1,0:T(8,128)} %index_ref.1, bf16[4,8,512]{2,1,0:T(8,128)(2,1)} %edges_ref.1, s32[8,512]{1,0:T(8,128)} %receive_ref.1, bf16[4,512]{1,0:T(4,128)(2,1)} %feature_ref.1, s32[16,32]{1,0:T(8,128)} %bitcast.7, s32[20,128]{1,0:T(8,128)} %bitcast.5, s32[20,128]{1,0:T(8,128)} %bitcast.6, ...), custom_call_target="tpu_custom_call" | custom-call | tf_op jit(solution)/shard_map/step/pallas_call | solution.py:574
  81.4 1.7 %copy.27 = bf16[320,512]{1,0:T(8,128)(2,1)} copy(bf16[320,512]{1,0:T(8,128)(2,1)} %step.1) | data formatting | bytes 655360

commit v4 on v3

--- a/solution.py
+++ b/solution.py
@@ -57,17 +57,18 @@
     return jnp.where(lax.rem(place, 2) == 1, ahead, lax.rem(subs // 2 + half, subs))
 
 
-def flip(index, mask, count):
-    total, bit = 0, 1
-    while bit < count:
-        total = total + lax.rem(lax.rem(index // bit, 2) + lax.rem(mask // bit, 2), 2) * bit
-        bit *= 2
-    return total
-
-
-def partner(step, faces, subs):
-    face, sub = lax.axis_index("face"), lax.axis_index("sub")
-    return flip(face, lax.rem(step, faces), faces), flip(sub, step // faces, subs)
+def flips(index, count):
+    bits = [(bit, lax.rem(lax.div(index, 1 << bit), 2)) for bit in range((count - 1).bit_length())]
+    return [
+        sum((((1 - value) if mask >> bit & 1 else value) << bit for bit, value in bits), 0)
+        for mask in range(count)
+    ]
+
+
+def partners(faces, subs):
+    face = flips(lax.axis_index("face"), faces)
+    sub = flips(lax.axis_index("sub"), subs)
+    return [(face[step % faces], sub[step // faces]) for step in range(faces * subs - 1, 0, -1)]
 
 
 def digits(values):
@@ -161,11 +162,9 @@
     here = ring_position(subs)
     barrier = pltpu.get_barrier_semaphore()
 
-    @pl.loop(1, faces * subs)
-    def _(step):
-        pl.semaphore_signal(
-            barrier, inc=1, device_id=partner(step, faces, subs), device_id_type=MESH_ID
-        )
+    others = partners(faces, subs)
+    for other in others:
+        pl.semaphore_signal(barrier, inc=1, device_id=other, device_id_type=MESH_ID)
 
     devices = faces * subs
     me = lax.axis_index("face") * subs + lax.axis_index("sub")
@@ -205,21 +204,6 @@
 
     for place in range(len(weights)):
         fetch(place).start()
-
-    high, low = digits(receive_ref[...])
-    features = [edges_ref[feat].astype(jnp.float32) for feat in range(feats)]
-    fill = jnp.zeros((8 - feats - 2, capacity), jnp.float32)
-    for sub in range(subs):
-        span = slice(sub, sub + 1)
-        stack = jnp.concatenate(
-            [feature[span, :] for feature in features] + [high[span, :], low[span, :], fill], axis=0
-        )
-        aux[sub] = jnp.concatenate(
-            [stack[:, : capacity // 2], stack[:, capacity // 2 :]], axis=0
-        ).astype(jnp.bfloat16)
-    table[0] = jnp.zeros((parts, LANES), jnp.float32)
-    wide_table[count:, :] = jnp.zeros((16, width), jnp.bfloat16)
-    wide_table[count : count + feats, :] = feature_ref[...]
 
     loads[0].wait()
     loads[1].wait()
@@ -259,6 +243,21 @@
     for part in range(2):
         for flow in range(2):
             gather(flow, 0, part).start()
+    high, low = digits(receive_ref[...])
+    features = [edges_ref[feat].astype(jnp.float32) for feat in range(feats)]
+    fill = jnp.zeros((8 - feats - 2, capacity), jnp.float32)
+    for sub in range(subs):
+        span = slice(sub, sub + 1)
+        stack = jnp.concatenate(
+            [feature[span, :] for feature in features] + [high[span, :], low[span, :], fill], axis=0
+        )
+        aux[sub] = jnp.concatenate(
+            [stack[:, : capacity // 2], stack[:, capacity // 2 :]], axis=0
+        ).astype(jnp.bfloat16)
+    table[0] = jnp.zeros((parts, LANES), jnp.float32)
+    wide_table[count:, :] = jnp.zeros((16, width), jnp.bfloat16)
+    wide_table[count : count + feats, :] = feature_ref[...]
+
     for distance in range(1, subs):
         side(distance).start()
     aux_in[0] = aux[sub_at(here, subs)]
@@ -393,6 +392,9 @@
             def _():
                 for action in waits[2 * when + 1] + events[when]:
                     action()
+
+    push_early(1)
+    push_late(1)
 
     edges = target_ref.shape[0] * LANES
     slots, table_slots = halo_ref.shape[0], halo_ref.shape[0] * devices
@@ -420,8 +422,6 @@
     arrived[pl.ds(pl.multiple_of(me * slots, slots), slots), :] = jnp.zeros(
         (slots, width), jnp.bfloat16
     )
-    push_early(1)
-
     high, low = digits(target[...])
     info = jnp.concatenate(
         [
@@ -441,7 +441,6 @@
         chosen = hot(index.astype(jnp.int32), count)
         found[span, :] = jnp.concatenate([chosen, read[:, :16].astype(jnp.bfloat16)], axis=1)
         spots[:, span] = chosen.T
-    push_late(1)
     local_table[2 * count :, :] = jnp.zeros((16, width), jnp.bfloat16)
     local_table[2 * count : 2 * count + feats, :] = tag_feature_ref[...]
 
@@ -462,7 +461,7 @@
         outgoing[span, :] = dot(leaving[span, :], state).astype(jnp.bfloat16)
 
     def copy(step):
-        face, sub = partner(step, faces, subs)
+        face, sub = others[step]
         other = face * subs + sub
         return pltpu.make_async_remote_copy(
             src_ref=outgoing.at[pl.ds(pl.multiple_of(other * slots, slots), slots), :],
@@ -473,9 +472,8 @@
             device_id_type=MESH_ID,
         )
 
-    @pl.loop(1, devices)
-    def _(step):
-        copy(devices - step).start()
+    for step in range(devices - 1):
+        copy(step).start()
 
     local_table[:count, :] = dot(state, weight(3)).astype(jnp.bfloat16)
     local_table[count : 2 * count, :] = dot(state, weight(4)).astype(jnp.bfloat16)
@@ -507,9 +505,8 @@
     fetch(7).wait()
     fetch(8).wait()
 
-    @pl.loop(1, devices)
-    def _(step):
-        copy(devices - step).wait()
+    for step in range(devices - 1):
+        copy(step).wait()
 
     for start in range(0, table_slots, group):
         span = slice(start, start + group)

time: 83.4 us -> 81.5 us (0.977)
  Pallas kernels: 81.4 us -> 79.6 us
    pallas_call x1, Pallas kernels: 81.4 us -> 79.6 us  [shards(): pl.pallas_call(functools.partial(step_kernel, rows, min(512, edge_count),...]
where the time goes in v4:
time: 81.5 us; the launch traced here: 81.3 us
  Pallas kernels  79.6 us (98%)
  local copies, waits for them, and re-layouts  1.72 us (2%)
    pallas_call x1, Pallas kernels, shards(): pl.pallas_call(functools.partial(step_kernel, rows, min(512, edge_count),...  79.6 us
    unnamed x1, local copies, waits for them, and re-layouts  1.72 us

profile of v4, /device:TPU:0, one launch (start us, length us, event | category | flops | bytes accessed | tf_op | source)
XLA Modules:
  0.0 81.3 jit_solution(11152698647830356321)
XLA Ops:
  0.0 79.6 %step.1 = bf16[320,512]{1,0:T(8,128)(2,1)} custom-call(s32[8,512]{1,0:T(8,128)} %index_ref.1, bf16[4,8,512]{2,1,0:T(8,128)(2,1)} %edges_ref.1, s32[8,512]{1,0:T(8,128)} %receive_ref.1, bf16[4,512]{1,0:T(4,128)(2,1)} %feature_ref.1, s32[16,32]{1,0:T(8,128)} %bitcast.7, s32[20,128]{1,0:T(8,128)} %bitcast.5, s32[20,128]{1,0:T(8,128)} %bitcast.6, ...), custom_call_target="tpu_custom_call" | custom-call | tf_op jit(solution)/shard_map/step/pallas_call | solution.py:571
  79.6 1.7 %copy.27 = bf16[320,512]{1,0:T(8,128)(2,1)} copy(bf16[320,512]{1,0:T(8,128)(2,1)} %step.1) | data formatting | bytes 655360
